TPU v7x, 128 devices: a whole 4x4x4 slice. The times are simulated.
128 devices in a mesh: inp: 16 (over y, z_lo, core), tm: 8 (over z_hi, x).
Axes of the slice: x: 4, y: 4, z: 4 (z_hi: 2, z_lo: 2; z = z_hi * 2 + z_lo), core: 2. Of those that a mesh axis runs over, the one named last changes fastest.
Arguments:
- voltages: bfloat16 [1024, 524288], P('inp', 'tm'), may hold values from -6 to 6
- prototype: float32 [8, 1024], replicated, may hold values from -2 to 2
Outputs:
- correlation: bfloat16 [512, 2, 1024, 1024], P(('inp', 'tm'))
All inputs are finite; a program needn't handle non-finite values.
Results may differ from a plain program's by a relative error of at most 0.0065.
Values may be sent and summed in bfloat16 or wider, within the bound.
A program may use at most 128 MiB of HBM per device.

v0:
```python
import math

import jax
import jax.numpy as jnp
from jax import lax
from jax.sharding import PartitionSpec as P

TAPS = 8
SPEC_DEV = 64
FRAME = 1024


def shifted(block, axis, distance):
    devices = range(lax.axis_size(axis))
    route = [(i - distance, i) for i in devices if i - distance in devices]
    return lax.ppermute(block, axis, route)


def dft_table(frame):
    sample = jnp.arange(frame, dtype=jnp.int32)[:, None]
    column = jnp.arange(frame, dtype=jnp.int32)[None, :]
    phase = (sample * (column // 2) % frame).astype(jnp.float32) * (2.0 * math.pi / frame)
    table = jnp.where(column % 2 == 0, jnp.cos(phase), -jnp.sin(phase))
    return table.astype(jnp.bfloat16)


def channelize(frames, earlier, prototype):
    count = frames.shape[1]
    joined = jnp.concatenate([earlier, frames], axis=1)
    filtered = jnp.zeros(frames.shape, jnp.float32)
    for tap_index in range(TAPS):
        filtered = filtered + prototype[tap_index] * joined[
            :, tap_index : tap_index + count, :
        ].astype(jnp.float32)
    filtered = filtered.astype(jnp.bfloat16)
    dims = (((0,), (2,)), ((), ()))
    spectra = lax.dot_general(
        dft_table(frames.shape[2]), filtered, dims, preferred_element_type=jnp.float32
    )
    return spectra.astype(jnp.bfloat16)


def correlate(planes):
    real_part = planes[0]
    imag_part = planes[1]
    dims = (((1,), (1,)), ((), ()))
    real_real = lax.dot_general(real_part, real_part, dims, preferred_element_type=jnp.float32)
    imag_imag = lax.dot_general(imag_part, imag_part, dims, preferred_element_type=jnp.float32)
    imag_real = lax.dot_general(imag_part, real_part, dims, preferred_element_type=jnp.float32)
    real_gram = real_real + imag_imag
    imag_gram = imag_real - imag_real.T
    scales = lax.rsqrt(jnp.diagonal(real_gram) + 1e-06)
    outer = scales[:, None] * scales[None, :]
    return jnp.stack([real_gram * outer, imag_gram * outer]).astype(jnp.bfloat16)


def shards(voltages, prototype):
    inputs_here = voltages.shape[0]
    frames = voltages.reshape(inputs_here, SPEC_DEV, FRAME)
    earlier = shifted(frames[:, SPEC_DEV - TAPS + 1 :, :], "tm", 1)
    spectra = channelize(frames, earlier, prototype)
    groups_inp = lax.axis_size("inp")
    groups_tm = lax.axis_size("tm")
    width = FRAME // (groups_inp * groups_tm)
    turned = lax.all_to_all(
        lax.all_to_all(spectra, "inp", split_axis=0, concat_axis=1, tiled=True),
        "tm",
        split_axis=0,
        concat_axis=2,
        tiled=True,
    )
    channels_here = width // 2
    planes = turned.reshape(channels_here, 2, turned.shape[1], turned.shape[2])
    return lax.map(correlate, planes)


def solution(mesh):
    return jax.shard_map(
        shards,
        mesh=mesh,
        in_specs=(P("inp", "tm"), P()),
        out_specs=P(("inp", "tm"), None, None, None),
        check_vma=False,
    )
```

profile of v0, /device:TPU:38, one launch (start us, length us, event | category | flops | bytes accessed | tf_op | source)
XLA Modules:
  0.0 620.4 jit_solution(17290612692274627774)
XLA Ops:
  0.0 0.0 copy-start
  0.0 11.8 %copy.24 = bf16[8,8,64,1024]{3,2,1,0:T(8,128)(2,1)} copy(bf16[8,8,64,1024]{3,1,2,0:T(8,128)(2,1)} %bitcast.71) | data formatting | bytes 16777216
  11.8 1.5 slice.74
  13.3 0.6 copy.15
  13.9 5.0 collective-permute-start
  18.9 0.0 copy-done
  18.9 17.0 %fusion.46 = bf16[1024,1024,1]{1,0,2:T(8,128)(2,1)S(1)} fusion(s32[1024]{0:T(1024)S(1)} %add_select_fusion.1, pred[1024]{0:T(1024)(128)(4,1)S(1)} %fusion.31), kind=kLoop, calls=%fused_computation.49.clone.clone.2 | loop fusion | flops 17825792 | bytes 2102272 | tf_op jit(solution)/shard_map/dot_general | solution.py:37
  35.9 2.4 collective-permute-done
  38.3 0.5 copy.16
  38.8 47.4 %fusion.16 = bf16[1024,64,64]{0,2,1:T(8,128)(2,1)} fusion(bf16[64,64,1024]{2,1,0:T(8,128)(2,1)} %bitcast.70, bf16[64,7,1024]{2,1,0:T(8,128)(2,1)S(1)} %copy.16, f32[1024]{0:T(1024)S(1)} %bitcast.78, f32[1024]{0:T(1024)S(1)} %bitcast.79, f32[1024]{0:T(1024)S(1)} %bitcast.73, f32[1024]{0:T(1024)S(1)} %bitcast.74, f32[1024]{0:T(1024)S(1)} %bitcast.75, ...), kind=kOutput, calls=%fused_computation.38 | convolution fusion | flops 8782872576 | bytes 19824640 | tf_op jit(solution)/shard_map/dot_general | solution.py:37
  86.2 23.9 %copy.17 = bf16[1024,64,64]{2,1,0:T(8,128)(2,1)} copy(bf16[1024,64,64]{0,2,1:T(8,128)(2,1)} %fusion.16) | data formatting | bytes 16777216 | tf_op jit(solution)/shard_map/convert_element_type | solution.py:40
  110.1 19.7 %reshape.123 = bf16[16,2,131072]{2,1,0:T(2,128)(2,1)} reshape(bf16[1024,64,64]{2,1,0:T(8,128)(2,1)} %copy.17) | data formatting | bytes 16777216
  129.8 99.6 %all_to_all.33 = bf16[16,2,131072]{2,1,0:T(2,128)(2,1)} all-to-all(bf16[16,2,131072]{2,1,0:T(2,128)(2,1)} %reshape.123), channel_id=1, replica_groups=mesh['inp'=16,'tm'=8] {'inp'}, dimensions={0} | all-to-all | bytes 16777216 | tf_op jit(solution)/shard_map/all_to_all | solution.py:66
  229.4 19.2 %reshape.124 = bf16[1024,64,64]{2,1,0:T(8,128)(2,1)} reshape(bf16[16,2,131072]{2,1,0:T(2,128)(2,1)} %all_to_all.33) | data formatting | bytes 16777216
  248.6 23.3 %copy.18 = bf16[16,64,64,64]{2,0,3,1:T(8,128)(2,1)} copy(bf16[16,64,64,64]{3,2,1,0:T(8,128)(2,1)} %bitcast.67) | data formatting | bytes 16777216 | tf_op jit(solution)/shard_map/all_to_all | solution.py:66
  271.9 22.6 %all_to_all.27 = bf16[64,1024,64]{1,2,0:T(8,128)(2,1)} reshape(bf16[64,16,64,64]{2,1,3,0:T(8,128)(2,1)} %bitcast.68) | data formatting | bytes 16777216 | tf_op jit(solution)/shard_map/all_to_all | solution.py:66
  294.5 7.9 %all-to-all-start.1 = ((bf16[64,1024,64]{1,2,0:T(8,128)(2,1)}), bf16[64,1024,64]{1,2,0:T(8,128)(2,1)}, u32[]{:S(2)}, u32[]{:S(2)}) async-start(bf16[64,1024,64]{1,2,0:T(8,128)(2,1)} %all_to_all.27), calls=%async_computation.1 | async-start | bytes 16777216 | tf_op jit(solution)/shard_map/all_to_all | solution.py:65
  302.4 125.1 %all-to-all-done.1 = bf16[64,1024,64]{1,2,0:T(8,128)(2,1)} async-done(((bf16[64,1024,64]{1,2,0:T(8,128)(2,1)}), bf16[64,1024,64]{1,2,0:T(8,128)(2,1)}, u32[]{:S(2)}, u32[]{:S(2)}) %all-to-all-start.1) | async-done | bytes 8388640 | tf_op jit(solution)/shard_map/all_to_all | solution.py:65
  427.5 8.4 %copy.19 = bf16[8,1024,8,64]{1,3,2,0:T(8,128)(2,1)} copy(bf16[8,1024,8,64]{1,3,0,2:T(8,128)(2,1)} %bitcast.18) | data formatting | bytes 16777216 | tf_op jit(solution)/shard_map/all_to_all | solution.py:65
  435.9 184.5 %while.10 = (s32[]{:T(128)}, bf16[4,2,1024,1024]{3,2,1,0:T(8,128)(2,1)}, bf16[4,2,1024,512]{2,3,1,0:T(8,128)(2,1)}, s32[]{:T(128)}, s32[]{:T(128)}, /*index=5*/s32[]{}) while((s32[]{:T(128)}, bf16[4,2,1024,1024]{3,2,1,0:T(8,128)(2,1)}, bf16[4,2,1024,512]{2,3,1,0:T(8,128)(2,1)}, s32[]{:T(128)}, s32[]{:T(128)}, /*index=5*/s32[]{}) %tuple.34), condition=%wide.region_1.2_spmd, body=%wide.region_0.1_spmd.sunk | while | flops 3236959232 | bytes 54561368 | solution.py:74
  435.9 4.8 fusion.51
  440.7 6.1 convolution_add_fusion.2
  446.8 17.1 %gather_fusion = f32[1024]{0:T(1024)S(1)} fusion(f32[1024,1024]{1,0:T(8,128)} %convolution_add_fusion.2, s32[1024]{0:T(1024)S(1)} %bitcast.65), kind=kCustom, calls=%fused_computation.clone.1 | custom fusion | bytes 16384 | tf_op jit(solution)/shard_map/while/body/eval_jaxpr/jit(diagonal)/cond/branch_0_fun/gather | solution.py:52
  464.0 4.8 fusion.52
  468.8 5.3 copy.26
  474.1 5.5 fusion.53
  479.6 2.5 maximum_dynamic-update-slice_fusion.2
  482.0 4.8 fusion.51
  486.8 6.1 convolution_add_fusion.2
  492.9 17.1 %gather_fusion = f32[1024]{0:T(1024)S(1)} fusion(f32[1024,1024]{1,0:T(8,128)} %convolution_add_fusion.2, s32[1024]{0:T(1024)S(1)} %bitcast.65), kind=kCustom, calls=%fused_computation.clone.1 | custom fusion | bytes 16384 | tf_op jit(solution)/shard_map/while/body/eval_jaxpr/jit(diagonal)/cond/branch_0_fun/gather | solution.py:52
  510.1 4.8 fusion.52
  514.9 5.3 copy.26
  520.2 5.5 fusion.53
  525.7 2.5 maximum_dynamic-update-slice_fusion.2
  528.2 4.8 fusion.51
  532.9 6.1 convolution_add_fusion.2
  539.0 17.1 %gather_fusion = f32[1024]{0:T(1024)S(1)} fusion(f32[1024,1024]{1,0:T(8,128)} %convolution_add_fusion.2, s32[1024]{0:T(1024)S(1)} %bitcast.65), kind=kCustom, calls=%fused_computation.clone.1 | custom fusion | bytes 16384 | tf_op jit(solution)/shard_map/while/body/eval_jaxpr/jit(diagonal)/cond/branch_0_fun/gather | solution.py:52
  556.2 4.8 fusion.52
  561.0 5.3 copy.26
  566.3 5.5 fusion.53
  571.8 2.5 maximum_dynamic-update-slice_fusion.2
  574.3 4.8 fusion.51
  579.1 6.1 convolution_add_fusion.2
  585.1 17.1 %gather_fusion = f32[1024]{0:T(1024)S(1)} fusion(f32[1024,1024]{1,0:T(8,128)} %convolution_add_fusion.2, s32[1024]{0:T(1024)S(1)} %bitcast.65), kind=kCustom, calls=%fused_computation.clone.1 | custom fusion | bytes 16384 | tf_op jit(solution)/shard_map/while/body/eval_jaxpr/jit(diagonal)/cond/branch_0_fun/gather | solution.py:52
  602.3 4.8 fusion.52
  607.1 5.3 copy.26
  612.5 5.5 fusion.53
  617.9 2.5 maximum_dynamic-update-slice_fusion.2
  (12 shorter events, 0.1 us)
Async XLA Ops:
  0.0 18.9 %copy-start = (f32[8,1024]{1,0:T(8,128)S(1)}, f32[8,1024]{1,0:T(8,128)}, u32[]{:S(2)}) copy-start(f32[8,1024]{1,0:T(8,128)} %param.5) | copy-start | bytes 98308
  13.9 24.4 %collective-permute-start = (bf16[64,7,1024]{2,0,1:T(8,128)(2,1)S(1)}, bf16[64,7,1024]{2,0,1:T(8,128)(2,1)S(1)}, u32[]{:S(2)}, u32[]{:S(2)}) collective-permute-start(bf16[64,7,1024]{2,0,1:T(8,128)(2,1)S(1)} %copy.15), channel_id=1, source_target_pairs={{0,1},{1,2},{2,3},{3,4},{4,5},{5,6},{6,7},{8,9},{9,10},{10,11},{11... | collective-permute-start | bytes 2752520 | tf_op jit(solution)/shard_map/ppermute | solution.py:16
  294.5 133.0 %all-to-all-start.1 = ((bf16[64,1024,64]{1,2,0:T(8,128)(2,1)}), bf16[64,1024,64]{1,2,0:T(8,128)(2,1)}, u32[]{:S(2)}, u32[]{:S(2)}) async-start(bf16[64,1024,64]{1,2,0:T(8,128)(2,1)} %all_to_all.27), calls=%async_computation.1 | async-start | bytes 16777216 | tf_op jit(solution)/shard_map/all_to_all | solution.py:65
where the time goes:
time: 626 us; the launch traced here: 620 us
  local copies, waits for them, and re-layouts  221 us (35%)
  waiting for transfers between devices  127 us (20%)
  matrix products  110 us (18%)
  blocking collectives  99.6 us (16%)
  other arithmetic  48.7 us (8%)
  starting transfers between devices  12.9 us (2%)
    all_to_all x1, waiting for transfers between devices, shards(): lax.all_to_all(lax.all_to_all(spectra, 'inp', split_axis=0, concat_axis=1...  125 us
    all_to_all x1, blocking collectives, shards(): lax.all_to_all(spectra, 'inp', split_axis=0, concat_axis=1, tiled=True)  99.6 us
    gather x4, local copies, waits for them, and re-layouts, correlate(): scales = lax.rsqrt(jnp.diagonal(real_gram) + 1e-06)  68.6 us
    unnamed x5, local copies, waits for them, and re-layouts  50.7 us
    dot_general x1, matrix products, channelize(): lax.dot_general(dft_table(frames.shape[2]), filtered, dims, preferred_ele...  47.4 us
    all_to_all x2, local copies, waits for them, and re-layouts, shards(): lax.all_to_all(spectra, 'inp', split_axis=0, concat_axis=1, tiled=True)  45.9 us
    dot_general x4, matrix products, correlate(): lax.dot_general(imag_part, imag_part, dims, preferred_element_type=jnp.fl...  24.3 us
    convert_element_type x1, local copies, waits for them, and re-layouts, channelize(): return spectra.astype(jnp.bfloat16)  23.9 us
  transfers between devices with their start and end apart: 2, of which 2 were waited for; matrix products, arithmetic and copies ran while one was open for 3% of the time, Pallas kernels for 0%

commit v1 on v0

v1 whole, which is shorter than its diff:
```python
import functools
import math

import jax
import jax.numpy as jnp
import numpy as np
from jax import lax
from jax.experimental import pallas as pl
from jax.experimental.pallas import tpu as pltpu
from jax.sharding import PartitionSpec as P

TAPS = 8
HALO = TAPS - 1
FRAME = 1024
INPUTS_DEV = 64
SPEC_DEV = 64
DEVICES = 128
GROUPS = 4
INP = 16
TM = 8
PAIRS = SPEC_DEV // 2
MESH = pl.DeviceIdType.MESH


def dft_rows():
    channel = np.arange(DEVICES)[None, :] * GROUPS + np.arange(GROUPS)[:, None]
    sample = np.arange(FRAME)
    phase = (channel[:, :, None] * sample % FRAME) * (2.0 * math.pi / FRAME)
    table = np.stack([np.cos(phase), -np.sin(phase)], axis=2)
    return table.reshape(GROUPS, 2 * DEVICES, FRAME).astype(jnp.bfloat16)


def channelize_kernel(
    v_hbm, proto_ref, table_hbm, r_hbm,
    v, table, filtered, turned, outbox,
    v_sem, table_sem, own_sem, halo_sems, send_sems, recv_sems,
):
    a = lax.axis_index("inp")
    b = lax.axis_index("tm")
    me = a * TM + b
    barrier = pltpu.get_barrier_semaphore()

    def place(k):
        other = lax.rem(me + k, DEVICES)
        return other, {"inp": other // TM, "tm": lax.rem(other, TM)}

    @pl.loop(1, DEVICES)
    def _(k):
        _, where = place(k)
        pl.semaphore_signal(barrier, inc=1, device_id=where, device_id_type=MESH)

    body = HALO * FRAME
    loads = [
        pltpu.make_async_copy(
            v_hbm.at[pl.ds(q * 16, 16), :],
            v.at[pl.ds(q * 16, 16), pl.ds(body, SPEC_DEV * FRAME)],
            v_sem.at[q],
        )
        for q in range(4)
    ]
    for load in loads:
        load.start()
    table_load = pltpu.make_async_copy(table_hbm, table, table_sem)
    table_load.start()

    def fir(q, chunk):
        @pl.loop(0, FRAME // 128)
        def _(nb):
            lanes = pl.multiple_of(nb * 128, 128)
            taps = [proto_ref[k : k + 1, pl.ds(lanes, 128)] for k in range(TAPS)]
            x = [
                v[
                    pl.ds(q * 16, 16),
                    pl.ds(pl.multiple_of((chunk * 8 + f) * FRAME + lanes, 128), 128),
                ].astype(jnp.float32)
                for f in range(8 + HALO)
            ]
            for s in range(8):
                total = taps[0] * x[s]
                for k in range(1, TAPS):
                    total = total + taps[k] * x[s + k]
                filtered[chunk * 8 + s, pl.ds(q * 16, 16), pl.ds(lanes, 128)] = total.astype(
                    jnp.bfloat16
                )

    halo = pltpu.make_async_remote_copy(
        src_ref=v_hbm.at[:, pl.ds((SPEC_DEV - HALO) * FRAME, body)],
        dst_ref=v.at[:, pl.ds(0, body)],
        send_sem=halo_sems.at[0],
        recv_sem=halo_sems.at[1],
        device_id={"tm": lax.rem(b + 1, TM)},
        device_id_type=MESH,
    )
    for q in range(4):
        loads[q].wait()
        pl.loop(1, 8)(functools.partial(fir, q))
        if q == 0:
            pl.semaphore_wait(barrier, DEVICES - 1)

            @pl.when(b < TM - 1)
            def _():
                halo.start()

    @pl.when(b == 0)
    def _():
        @pl.loop(0, HALO)
        def _(f):
            v[:, pl.ds(pl.multiple_of(f * FRAME, FRAME), FRAME)] = jnp.zeros(
                (INPUTS_DEV, FRAME), jnp.bfloat16
            )

    @pl.when(b > 0)
    def _():
        halo.wait_recv()

    for q in range(4):
        fir(q, 0)
    table_load.wait()

    @pl.loop(0, GROUPS)
    def _(j):
        rows = table.at[j]

        @pl.loop(0, 8)
        def _(cb):
            block = filtered[pl.ds(cb * 8, 8)].reshape(8 * INPUTS_DEV, FRAME)
            out = lax.dot_general(
                rows[...], block, (((1,), (1,)), ((), ())), preferred_element_type=jnp.float32
            )
            for l in range(4):
                turned[pl.ds(cb * 4 + l, 2 * DEVICES, stride=PAIRS), :] = out[
                    :, l * 128 : (l + 1) * 128
                ]

        @pl.loop(0, 32)
        def _(r):
            outbox[j, pl.ds(r * 4, 4)] = (
                turned[pl.ds(pl.multiple_of(r * 256, 256), 256), :]
                .astype(jnp.bfloat16)
                .reshape(4, 2, PAIRS, 128)
            )

        pltpu.make_async_copy(
            outbox.at[j, me], r_hbm.at[j, a, :, pl.ds(b * PAIRS, PAIRS), :], own_sem.at[j]
        ).start()

        @pl.loop(1, DEVICES)
        def _(k):
            other, where = place(k)
            pltpu.make_async_remote_copy(
                src_ref=outbox.at[j, other],
                dst_ref=r_hbm.at[j, a, :, pl.ds(b * PAIRS, PAIRS), :],
                send_sem=send_sems.at[j],
                recv_sem=recv_sems.at[j],
                device_id=where,
                device_id_type=MESH,
            ).start()

    @pl.when(b < TM - 1)
    def _():
        halo.wait_send()

    @pl.loop(0, GROUPS)
    def _(j):
        pltpu.make_async_copy(
            outbox.at[j, me], r_hbm.at[j, a, :, pl.ds(b * PAIRS, PAIRS), :], own_sem.at[j]
        ).wait()
        sent = outbox.at[j, pl.ds(0, DEVICES - 1)]
        pltpu.make_async_copy(sent, sent, send_sems.at[j]).wait()
        pltpu.make_async_copy(sent, sent, recv_sems.at[j]).wait()


def channelize(voltages, prototype, table):
    return pl.pallas_call(
        channelize_kernel,
        out_shape=jax.ShapeDtypeStruct((GROUPS, INP, 2, TM * PAIRS, 128), jnp.bfloat16),
        in_specs=[
            pl.BlockSpec(memory_space=pl.ANY),
            pl.BlockSpec(memory_space=pltpu.VMEM),
            pl.BlockSpec(memory_space=pl.ANY),
        ],
        out_specs=pl.BlockSpec(memory_space=pl.ANY),
        scratch_shapes=[
            pltpu.VMEM((INPUTS_DEV, (SPEC_DEV + HALO) * FRAME), jnp.bfloat16),
            pltpu.VMEM((GROUPS, 2 * DEVICES, FRAME), jnp.bfloat16),
            pltpu.VMEM((SPEC_DEV, INPUTS_DEV, FRAME), jnp.bfloat16),
            pltpu.VMEM((2 * DEVICES * PAIRS, 128), jnp.float32),
            pltpu.VMEM((GROUPS, DEVICES, 2, PAIRS, 128), jnp.bfloat16),
            pltpu.SemaphoreType.DMA((4,)),
            pltpu.SemaphoreType.DMA,
            pltpu.SemaphoreType.DMA((GROUPS,)),
            pltpu.SemaphoreType.DMA((2,)),
            pltpu.SemaphoreType.DMA((GROUPS,)),
            pltpu.SemaphoreType.DMA((GROUPS,)),
        ],
        compiler_params=pltpu.CompilerParams(
            collective_id=0, has_side_effects=True, vmem_limit_bytes=56 * 1024 * 1024
        ),
        name="channelize",
    )(voltages, prototype, table)


def correlate_kernel(r_ref, o_ref, y, yt, scale_col, scale_row):
    step = pl.program_id(1)
    half = TM * PAIRS

    @pl.when(step == 0)
    def _():
        low = lax.broadcasted_iota(jnp.int32, (half, 128), 1) < 64
        for q in range(INP // 2):
            power = jnp.zeros((1, 128), jnp.float32)
            for p in range(2):
                even = r_ref[0, 2 * q, p].astype(jnp.float32)
                odd = r_ref[0, 2 * q + 1, p].astype(jnp.float32)
                first = jnp.where(low, even, pltpu.roll(odd, 64, 1))
                second = jnp.where(low, pltpu.roll(even, 64, 1), odd)
                power = power + jnp.sum(first * first + second * second, axis=0, keepdims=True)
                for h, part in enumerate((first, second)):
                    part = part.astype(jnp.bfloat16)
                    base = (2 * p + h) * half
                    y[base : base + half, q * 128 : (q + 1) * 128] = part
                    yt[q * 128 : (q + 1) * 128, base : base + half] = part.T
            scale = lax.rsqrt(power + 1e-06)
            scale_row[:, q * 128 : (q + 1) * 128] = scale
            scale_col[q * 128 : (q + 1) * 128, :] = jnp.broadcast_to(scale, (128, 128)).T

    rows = pl.ds(pl.multiple_of(step * 256, 256), 256)
    left = yt[rows, :]
    right = jnp.concatenate([left[:, 2 * half :], -left[:, : 2 * half]], axis=1)
    column = scale_col[rows, 0:1]
    for n in range(4):
        cols = slice(n * 256, (n + 1) * 256)
        outer = column * scale_row[:, cols]
        gram = jnp.dot(left, y[:, cols], preferred_element_type=jnp.float32)
        o_ref[0, 0, :, cols] = (gram * outer).astype(jnp.bfloat16)
        gram = jnp.dot(right, y[:, cols], preferred_element_type=jnp.float32)
        o_ref[0, 1, :, cols] = (gram * outer).astype(jnp.bfloat16)


def correlate(received):
    return pl.pallas_call(
        correlate_kernel,
        grid=(GROUPS, 4),
        out_shape=jax.ShapeDtypeStruct((GROUPS, 2, 1024, 1024), jnp.bfloat16),
        in_specs=[
            pl.BlockSpec((1, INP, 2, TM * PAIRS, 128), lambda c, i: (c, 0, 0, 0, 0)),
        ],
        out_specs=pl.BlockSpec((1, 2, 256, 1024), lambda c, i: (c, 0, i, 0)),
        scratch_shapes=[
            pltpu.VMEM((1024, 1024), jnp.bfloat16),
            pltpu.VMEM((1024, 1024), jnp.bfloat16),
            pltpu.VMEM((1024, 128), jnp.float32),
            pltpu.VMEM((1, 1024), jnp.float32),
        ],
        compiler_params=pltpu.CompilerParams(vmem_limit_bytes=48 * 1024 * 1024),
        name="correlate",
    )(received)


def shards(voltages, prototype):
    table = jnp.asarray(dft_rows())
    return correlate(channelize(voltages, prototype, table))


def solution(mesh):
    return jax.shard_map(
        shards,
        mesh=mesh,
        in_specs=(P("inp", "tm"), P()),
        out_specs=P(("inp", "tm"), None, None, None),
        check_vma=False,
    )
```

time: 626 us -> 175 us (0.28)
  the two profiles are of different devices: /device:TPU:38 before, /device:TPU:1 now
where the time goes in v1:
time: 175 us
  Pallas kernels  175 us (100%)
    pallas_call x1, Pallas kernels, channelize(): pl.pallas_call(channelize_kernel, out_shape=jax.ShapeDtypeStruct((GROUPS,...  141 us
    pallas_call x1, Pallas kernels, correlate(): pl.pallas_call(correlate_kernel, grid=(GROUPS, 4), out_shape=jax.ShapeDty...  33.7 us

profile of v1, /device:TPU:1, one launch (start us, length us, event | category | flops | bytes accessed | tf_op | source)
XLA Modules:
  0.0 175.1 jit_solution(10068542193121250694)
XLA Ops:
  0.0 141.4 %channelize.1.r_ref = bf16[4,16,2,256,128]{4,3,2,1,0:T(8,128)(2,1)} custom-call(bf16[64,65536]{1,0:T(8,128)(2,1)} %v_hbm.1, f32[8,1024]{1,0:T(8,128)} %proto_ref.1, bf16[4,256,1024]{2,1,0:T(8,128)(2,1)} %constant.2.clone.table_hbm), custom_call_target="tpu_custom_call" | custom-call | tf_op jit(solution)/shard_map/channelize/pallas_call | solution.py:174
  141.4 33.7 %correlate.1 = bf16[4,2,1024,1024]{3,2,1,0:T(8,128)(2,1)} custom-call(bf16[4,16,2,256,128]{4,3,2,1,0:T(8,128)(2,1)} %channelize.1.r_ref), custom_call_target="tpu_custom_call" | custom-call | tf_op jit(solution)/shard_map/correlate/pallas_call | solution.py:241

commit v2 on v1

v2 whole, which is shorter than its diff:
```python
import functools
import math

import jax
import jax.numpy as jnp
import numpy as np
from jax import lax
from jax.experimental import pallas as pl
from jax.experimental.pallas import tpu as pltpu
from jax.sharding import PartitionSpec as P

TAPS = 8
HALO = TAPS - 1
FRAME = 1024
INPUTS = 1024
INPUTS_DEV = 64
SPEC_DEV = 64
DEVICES = 128
GROUPS = 4
INP = 16
TM = 8
HALF = SPEC_DEV // 2
PAIRS = HALF // 2
STRIDE = PAIRS + 1
TILE = 256
MESH = pl.DeviceIdType.MESH


def dft_rows():
    channel = np.arange(DEVICES)[None, :] * GROUPS + np.arange(GROUPS)[:, None]
    sample = np.arange(FRAME)
    phase = (channel[:, :, None] * sample % FRAME) * (2.0 * math.pi / FRAME)
    table = np.stack([np.cos(phase), -np.sin(phase)], axis=2)
    return table.reshape(GROUPS, 2 * DEVICES, FRAME).astype(jnp.bfloat16)


def correlate_channel(received, rows, scale_col, scale_row, out):
    @pl.loop(0, INP)
    def _(a):
        at = pl.ds(pl.multiple_of(a * INPUTS_DEV, INPUTS_DEV), INPUTS_DEV)
        for p in range(2):
            turned = received[a, :, :, p].reshape(TM * HALF, 128).T
            for h in range(2):
                base = (2 * p + h) * TM * HALF
                rows[at, base : base + TM * HALF] = turned[h * 64 : (h + 1) * 64]

    half = INPUTS // 2

    def grams(left, right, n):
        other = rows[n * TILE : (n + 1) * TILE, :]
        dims = (((1,), (1,)), ((), ()))
        return (
            lax.dot_general(left, other, dims, preferred_element_type=jnp.float32),
            lax.dot_general(right, other, dims, preferred_element_type=jnp.float32),
        )

    def sides(m):
        left = rows[m * TILE : (m + 1) * TILE, :]
        return left, jnp.concatenate([left[:, half:], -left[:, :half]], axis=1)

    eye = lax.broadcasted_iota(jnp.int32, (TILE, TILE), 0) == lax.broadcasted_iota(
        jnp.int32, (TILE, TILE), 1
    )
    for m in range(INPUTS // TILE):
        at = slice(m * TILE, (m + 1) * TILE)
        real, imag = grams(*sides(m), m)
        diagonal = jnp.where(eye, real, 0.0)
        column = lax.rsqrt(jnp.sum(diagonal, axis=1, keepdims=True) + 1e-06)
        row = lax.rsqrt(jnp.sum(diagonal, axis=0, keepdims=True) + 1e-06)
        scale_col[at, :] = jnp.broadcast_to(column, (TILE, 128))
        scale_row[:, at] = row
        outer = column * row
        out[0, at, at] = (real * outer).astype(jnp.bfloat16)
        out[1, at, at] = (imag * outer).astype(jnp.bfloat16)
    for m in range(INPUTS // TILE - 1):
        left, right = sides(m)
        at = slice(m * TILE, (m + 1) * TILE)
        column = scale_col[at, 0:1]
        for n in range(m + 1, INPUTS // TILE):
            to = slice(n * TILE, (n + 1) * TILE)
            outer = column * scale_row[:, to]
            real, imag = grams(left, right, n)
            real = (real * outer).astype(jnp.bfloat16)
            imag = (imag * outer).astype(jnp.bfloat16)
            out[0, at, to] = real
            out[1, at, to] = imag
            out[0, to, at] = real.T
            out[1, to, at] = -imag.T


def channelize_kernel(
    v_hbm, proto_ref, table_hbm, done_hbm, last_hbm,
    v, table, filtered, turned, outbox, inbox, rows, scale_col, scale_row, staged,
    v_sems, table_sem, own_sems, halo_sems, send_sems, recv_sems, done_sems,
):
    a = lax.axis_index("inp")
    b = lax.axis_index("tm")
    me = a * TM + b
    barrier = pltpu.get_barrier_semaphore()
    body = HALO * FRAME
    split = HALF * FRAME

    loads = [
        pltpu.make_async_copy(
            v_hbm.at[:, pl.ds(split - body, SPEC_DEV * FRAME - split + body)],
            v.at[:, pl.ds(split, SPEC_DEV * FRAME - split + body)],
            v_sems.at[1],
        ),
        pltpu.make_async_copy(
            v_hbm.at[:, pl.ds(0, split - body)], v.at[:, pl.ds(body, split - body)], v_sems.at[0]
        ),
    ]
    table_load = pltpu.make_async_copy(table_hbm, table, table_sem)
    loads[0].start()
    table_load.start()
    loads[1].start()

    def place(k):
        other = lax.rem(me + k * 37, DEVICES)
        return other, {"inp": lax.div(other, TM), "tm": lax.rem(other, TM)}

    @pl.loop(1, DEVICES)
    def _(k):
        _, where = place(k)
        pl.semaphore_signal(barrier, inc=1, device_id=where, device_id_type=MESH)

    def fir(t):
        chunk = lax.div(t, 4)
        at = pl.ds(pl.multiple_of(lax.rem(t, 4) * 16, 16), 16)
        for nb in range(FRAME // 128):
            lanes = slice(nb * 128, (nb + 1) * 128)
            taps = [proto_ref[k : k + 1, lanes] for k in range(TAPS)]
            x = [
                v[
                    at, pl.ds(pl.multiple_of((chunk * 8 + f) * FRAME + nb * 128, 128), 128)
                ].astype(jnp.float32)
                for f in range(8 + HALO)
            ]
            for s in range(8):
                total = taps[0] * x[s]
                for k in range(1, TAPS):
                    total = total + taps[k] * x[s + k]
                filtered[chunk * 8 + s, at, lanes] = total.astype(jnp.bfloat16)

    def dft(j, half):
        block = filtered[pl.ds(half * HALF, HALF)].reshape(HALF * INPUTS_DEV, FRAME)
        out = lax.dot_general(
            table[j], block, (((1,), (1,)), ((), ())), preferred_element_type=jnp.float32
        )
        for l in range(PAIRS):
            turned[pl.ds(l, 2 * DEVICES, stride=STRIDE), :] = out[:, l * 128 : (l + 1) * 128]
        for m in range(2 * DEVICES):
            outbox[j, m // 2, half, m % 2] = turned[pl.ds(m * STRIDE, PAIRS), :].astype(
                jnp.bfloat16
            )

    def send(j, source, target):
        @pl.loop(1, DEVICES)
        def _(k):
            other, where = place(k)
            pltpu.make_async_remote_copy(
                src_ref=source(other),
                dst_ref=target,
                send_sem=send_sems.at[j],
                recv_sem=recv_sems.at[j],
                device_id=where,
                device_id_type=MESH,
            ).start()

    halo = pltpu.make_async_remote_copy(
        src_ref=v_hbm.at[:, pl.ds((SPEC_DEV - HALO) * FRAME, body)],
        dst_ref=v.at[:, pl.ds(0, body)],
        send_sem=halo_sems.at[0],
        recv_sem=halo_sems.at[1],
        device_id={"tm": lax.rem(b + 1, TM)},
        device_id_type=MESH,
    )

    loads[0].wait()
    pl.loop(16, 32)(fir)
    table_load.wait()

    @pl.loop(0, 2)
    def _(j):
        dft(j, 1)

        @pl.when(j == 0)
        def _():
            pl.semaphore_wait(barrier, DEVICES - 1)

            @pl.when(b < TM - 1)
            def _():
                halo.start()

        send(j, lambda other: outbox.at[j, other, 1], inbox.at[j, a, b, 1])

    loads[1].wait()
    pl.loop(4, 16)(fir)

    @pl.when(b == 0)
    def _():
        @pl.loop(0, HALO)
        def _(f):
            v[:, pl.ds(pl.multiple_of(f * FRAME, FRAME), FRAME)] = jnp.zeros(
                (INPUTS_DEV, FRAME), jnp.bfloat16
            )

    @pl.when(b > 0)
    def _():
        halo.wait_recv()

    pl.loop(0, 4)(fir)

    @pl.loop(0, 2)
    def _(j):
        dft(j, 0)
        send(j, lambda other: outbox.at[j, other, 0], inbox.at[j, a, b, 0])

    @pl.loop(2, GROUPS)
    def _(j):
        @pl.loop(0, 2)
        def _(half):
            dft(j, half)

        @pl.when(j == 2)
        def _():
            send(2, lambda other: outbox.at[2, other], inbox.at[2, a, b])

        @pl.when(j == 3)
        def _():
            send(3, lambda other: outbox.at[3, other], last_hbm.at[a, b])

    owns = [
        pltpu.make_async_copy(
            outbox.at[j, me], inbox.at[j, a, b] if j < 3 else last_hbm.at[a, b], own_sems.at[j]
        )
        for j in range(GROUPS)
    ]
    for own in owns:
        own.start()

    @pl.when(b < TM - 1)
    def _():
        halo.wait_send()

    def arrived(j):
        some = outbox.at[j, pl.ds(0, DEVICES - 1)]
        pltpu.make_async_copy(some, some, recv_sems.at[j]).wait()

    def written(j):
        return pltpu.make_async_copy(staged.at[lax.rem(j, 2)], done_hbm.at[j], done_sems.at[j])

    for j in range(3):
        owns[j].wait()

    @pl.loop(0, 3)
    def _(j):
        arrived(j)

        @pl.when(j == 2)
        def _():
            written(0).wait()

        correlate_channel(inbox.at[j], rows, scale_col, scale_row, staged.at[lax.rem(j, 2)])
        written(j).start()

    written(1).wait()
    written(2).wait()
    owns[3].wait()
    arrived(3)

    @pl.loop(0, GROUPS)
    def _(j):
        some = outbox.at[j, pl.ds(0, DEVICES - 1)]
        pltpu.make_async_copy(some, some, send_sems.at[j]).wait()


def channelize(voltages, prototype, table):
    piece = (INP, TM, 2, 2, PAIRS, 128)
    return pl.pallas_call(
        channelize_kernel,
        out_shape=(
            jax.ShapeDtypeStruct((3, 2, INPUTS, INPUTS), jnp.bfloat16),
            jax.ShapeDtypeStruct(piece, jnp.bfloat16),
        ),
        in_specs=[
            pl.BlockSpec(memory_space=pl.ANY),
            pl.BlockSpec(memory_space=pltpu.VMEM),
            pl.BlockSpec(memory_space=pl.ANY),
        ],
        out_specs=(pl.BlockSpec(memory_space=pl.ANY), pl.BlockSpec(memory_space=pl.ANY)),
        scratch_shapes=[
            pltpu.VMEM((INPUTS_DEV, (SPEC_DEV + HALO) * FRAME), jnp.bfloat16),
            pltpu.VMEM((GROUPS, 2 * DEVICES, FRAME), jnp.bfloat16),
            pltpu.VMEM((SPEC_DEV, INPUTS_DEV, FRAME), jnp.bfloat16),
            pltpu.VMEM((2 * DEVICES * STRIDE, 128), jnp.float32),
            pltpu.VMEM((GROUPS, DEVICES, 2, 2, PAIRS, 128), jnp.bfloat16),
            pltpu.VMEM((3, *piece), jnp.bfloat16),
            pltpu.VMEM((INPUTS, INPUTS), jnp.bfloat16),
            pltpu.VMEM((INPUTS, 128), jnp.float32),
            pltpu.VMEM((1, INPUTS), jnp.float32),
            pltpu.VMEM((2, 2, INPUTS, INPUTS), jnp.bfloat16),
            pltpu.SemaphoreType.DMA((2,)),
            pltpu.SemaphoreType.DMA,
            pltpu.SemaphoreType.DMA((GROUPS,)),
            pltpu.SemaphoreType.DMA((2,)),
            pltpu.SemaphoreType.DMA((GROUPS,)),
            pltpu.SemaphoreType.DMA((GROUPS,)),
            pltpu.SemaphoreType.DMA((3,)),
        ],
        compiler_params=pltpu.CompilerParams(
            collective_id=0, has_side_effects=True, vmem_limit_bytes=60 * 1024 * 1024
        ),
        name="channelize",
    )(voltages, prototype, table)


def finish_kernel(
    done_hbm, last_hbm, o_hbm, received, rows, scale_col, scale_row, staged, sems, copy_sems
):
    load = pltpu.make_async_copy(last_hbm, received, sems.at[0])
    load.start()
    copies = [
        pltpu.make_async_copy(done_hbm.at[c, p], o_hbm.at[c, p], copy_sems.at[c, p])
        for c in range(3)
        for p in range(2)
    ]
    for copy in copies:
        copy.start()
    load.wait()
    correlate_channel(received, rows, scale_col, scale_row, staged)
    store = pltpu.make_async_copy(staged, o_hbm.at[3], sems.at[1])
    store.start()
    for copy in copies:
        copy.wait()
    store.wait()


def finish(done, last):
    return pl.pallas_call(
        finish_kernel,
        out_shape=jax.ShapeDtypeStruct((GROUPS, 2, INPUTS, INPUTS), jnp.bfloat16),
        in_specs=[pl.BlockSpec(memory_space=pl.ANY)] * 2,
        out_specs=pl.BlockSpec(memory_space=pl.ANY),
        scratch_shapes=[
            pltpu.VMEM((INP, TM, 2, 2, PAIRS, 128), jnp.bfloat16),
            pltpu.VMEM((INPUTS, INPUTS), jnp.bfloat16),
            pltpu.VMEM((INPUTS, 128), jnp.float32),
            pltpu.VMEM((1, INPUTS), jnp.float32),
            pltpu.VMEM((2, INPUTS, INPUTS), jnp.bfloat16),
            pltpu.SemaphoreType.DMA((2,)),
            pltpu.SemaphoreType.DMA((3, 2)),
        ],
        compiler_params=pltpu.CompilerParams(vmem_limit_bytes=60 * 1024 * 1024),
        name="finish",
    )(done, last)


def shards(voltages, prototype):
    table = jnp.asarray(dft_rows())
    return finish(*channelize(voltages, prototype, table))


def solution(mesh):
    return jax.shard_map(
        shards,
        mesh=mesh,
        in_specs=(P("inp", "tm"), P()),
        out_specs=P(("inp", "tm"), None, None, None),
        check_vma=False,
    )
```

time: 175 us -> 525 us (3.00)
  Pallas kernels: 175 us -> 524 us
    pallas_call x2, Pallas kernels: 175 us -> 524 us  [the longest x1 382 us: finish(): pl.pallas_call(finish_kernel, out_shape=jax.ShapeDtypeStruct((GROUPS, 2,...]
where the time goes in v2:
time: 525 us; the launch traced here: 524 us
  Pallas kernels  524 us (100%)
    pallas_call x1, Pallas kernels, finish(): pl.pallas_call(finish_kernel, out_shape=jax.ShapeDtypeStruct((GROUPS, 2,...  382 us
    pallas_call x1, Pallas kernels, channelize(): pl.pallas_call(channelize_kernel, out_shape=(jax.ShapeDtypeStruct((3, 2,...  141 us

profile of v2, /device:TPU:1, one launch (start us, length us, event | category | flops | bytes accessed | tf_op | source)
XLA Modules:
  0.0 523.8 jit_solution(15290557389933159898)
XLA Ops:
  0.0 141.4 %channelize.1 = (bf16[3,2,1024,1024]{3,2,1,0:T(8,128)(2,1)}, bf16[16,8,2,2,16,128]{5,4,3,2,1,0:T(8,128)(2,1)}) custom-call(bf16[64,65536]{1,0:T(8,128)(2,1)} %v_hbm.1, f32[8,1024]{1,0:T(8,128)} %proto_ref.1, bf16[4,256,1024]{2,1,0:T(8,128)(2,1)} %constant.2.clone.table_hbm), custom_call_target="tpu_custom_call" | custom-call | tf_op jit(solution)/shard_map/channelize/pallas_call | solution.py:280
  141.4 382.3 %finish.1 = bf16[4,2,1024,1024]{3,2,1,0:T(8,128)(2,1)} custom-call(bf16[3,2,1024,1024]{3,2,1,0:T(8,128)(2,1)} %get-tuple-element.7.done_hbm, bf16[16,8,2,2,16,128]{5,4,3,2,1,0:T(8,128)(2,1)} %get-tuple-element.8.last_hbm), custom_call_target="tpu_custom_call" | custom-call | tf_op jit(solution)/shard_map/finish/pallas_call | solution.py:340

commit v3 on v2

--- a/solution.py
+++ b/solution.py
@@ -11,6 +11,8 @@
 
 TAPS = 8
 HALO = TAPS - 1
+AFTER = HALO // 2
+BEFORE = HALO - AFTER
 FRAME = 1024
 INPUTS = 1024
 INPUTS_DEV = 64
@@ -97,23 +99,22 @@
     b = lax.axis_index("tm")
     me = a * TM + b
     barrier = pltpu.get_barrier_semaphore()
-    body = HALO * FRAME
-    split = HALF * FRAME
+
+    def frames(first, count):
+        return pl.ds(first * FRAME, count * FRAME)
 
     loads = [
         pltpu.make_async_copy(
-            v_hbm.at[:, pl.ds(split - body, SPEC_DEV * FRAME - split + body)],
-            v.at[:, pl.ds(split, SPEC_DEV * FRAME - split + body)],
-            v_sems.at[1],
-        ),
-        pltpu.make_async_copy(
-            v_hbm.at[:, pl.ds(0, split - body)], v.at[:, pl.ds(body, split - body)], v_sems.at[0]
-        ),
+            v_hbm.at[pl.ds(q * 16, 16), :],
+            v.at[pl.ds(q * 16, 16), frames(BEFORE, SPEC_DEV)],
+            v_sems.at[q],
+        )
+        for q in range(4)
     ]
+    for load in loads:
+        load.start()
     table_load = pltpu.make_async_copy(table_hbm, table, table_sem)
-    loads[0].start()
     table_load.start()
-    loads[1].start()
 
     def place(k):
         other = lax.rem(me + k * 37, DEVICES)
@@ -124,9 +125,10 @@
         _, where = place(k)
         pl.semaphore_signal(barrier, inc=1, device_id=where, device_id_type=MESH)
 
-    def fir(t):
-        chunk = lax.div(t, 4)
-        at = pl.ds(pl.multiple_of(lax.rem(t, 4) * 16, 16), 16)
+    def fir(chunk, q, last=False):
+        at = pl.ds(pl.multiple_of(q * 16, 16), 16)
+        slot = lax.rem(chunk + 6, 8) * 8
+        keep = jnp.where(b < TM - 1, 1.0, 0.0) if last else None
         for nb in range(FRAME // 128):
             lanes = slice(nb * 128, (nb + 1) * 128)
             taps = [proto_ref[k : k + 1, lanes] for k in range(TAPS)]
@@ -139,8 +141,10 @@
             for s in range(8):
                 total = taps[0] * x[s]
                 for k in range(1, TAPS):
+                    if last and s + k == 8 + BEFORE:
+                        total = total * keep
                     total = total + taps[k] * x[s + k]
-                filtered[chunk * 8 + s, at, lanes] = total.astype(jnp.bfloat16)
+                filtered[slot + s, at, lanes] = total.astype(jnp.bfloat16)
 
     def dft(j, half):
         block = filtered[pl.ds(half * HALF, HALF)].reshape(HALF * INPUTS_DEV, FRAME)
@@ -167,39 +171,40 @@
                 device_id_type=MESH,
             ).start()
 
-    halo = pltpu.make_async_remote_copy(
-        src_ref=v_hbm.at[:, pl.ds((SPEC_DEV - HALO) * FRAME, body)],
-        dst_ref=v.at[:, pl.ds(0, body)],
-        send_sem=halo_sems.at[0],
-        recv_sem=halo_sems.at[1],
-        device_id={"tm": lax.rem(b + 1, TM)},
-        device_id_type=MESH,
-    )
-
-    loads[0].wait()
-    pl.loop(16, 32)(fir)
+    def halo(first, count, to, step, n):
+        return pltpu.make_async_remote_copy(
+            src_ref=v.at[:, frames(first, count)],
+            dst_ref=v.at[:, frames(to, count)],
+            send_sem=halo_sems.at[n],
+            recv_sem=halo_sems.at[2 + n],
+            device_id={"tm": lax.rem(b + step, TM)},
+            device_id_type=MESH,
+        )
+
+    forward = halo(SPEC_DEV, BEFORE, 0, 1, 0)
+    back = halo(BEFORE, AFTER, BEFORE + SPEC_DEV, TM - 1, 1)
+    for load in loads:
+        load.wait()
+    pl.semaphore_wait(barrier, DEVICES - 1)
+    back.start()
+
+    @pl.when(b < TM - 1)
+    def _():
+        forward.start()
+
+    pl.loop(0, 16)(lambda t: fir(2 + lax.div(t, 4), lax.rem(t, 4)))
     table_load.wait()
 
     @pl.loop(0, 2)
     def _(j):
-        dft(j, 1)
-
-        @pl.when(j == 0)
-        def _():
-            pl.semaphore_wait(barrier, DEVICES - 1)
-
-            @pl.when(b < TM - 1)
-            def _():
-                halo.start()
-
-        send(j, lambda other: outbox.at[j, other, 1], inbox.at[j, a, b, 1])
-
-    loads[1].wait()
-    pl.loop(4, 16)(fir)
+        dft(j, 0)
+        send(j, lambda other: outbox.at[j, other, 0], inbox.at[j, a, b, 0])
+
+    pl.loop(0, 8)(lambda t: fir(6 - 5 * lax.div(t, 4), lax.rem(t, 4)))
 
     @pl.when(b == 0)
     def _():
-        @pl.loop(0, HALO)
+        @pl.loop(0, BEFORE)
         def _(f):
             v[:, pl.ds(pl.multiple_of(f * FRAME, FRAME), FRAME)] = jnp.zeros(
                 (INPUTS_DEV, FRAME), jnp.bfloat16
@@ -207,14 +212,16 @@
 
     @pl.when(b > 0)
     def _():
-        halo.wait_recv()
-
-    pl.loop(0, 4)(fir)
+        forward.wait_recv()
+
+    pl.loop(0, 4)(lambda q: fir(0, q))
+    back.wait_recv()
+    pl.loop(0, 4)(lambda q: fir(7, q, True))
 
     @pl.loop(0, 2)
     def _(j):
-        dft(j, 0)
-        send(j, lambda other: outbox.at[j, other, 0], inbox.at[j, a, b, 0])
+        dft(j, 1)
+        send(j, lambda other: outbox.at[j, other, 1], inbox.at[j, a, b, 1])
 
     @pl.loop(2, GROUPS)
     def _(j):
@@ -239,9 +246,11 @@
     for own in owns:
         own.start()
 
+    back.wait_send()
+
     @pl.when(b < TM - 1)
     def _():
-        halo.wait_send()
+        forward.wait_send()
 
     def arrived(j):
         some = outbox.at[j, pl.ds(0, DEVICES - 1)]
@@ -300,10 +309,10 @@
             pltpu.VMEM((INPUTS, 128), jnp.float32),
             pltpu.VMEM((1, INPUTS), jnp.float32),
             pltpu.VMEM((2, 2, INPUTS, INPUTS), jnp.bfloat16),
-            pltpu.SemaphoreType.DMA((2,)),
+            pltpu.SemaphoreType.DMA((4,)),
             pltpu.SemaphoreType.DMA,
             pltpu.SemaphoreType.DMA((GROUPS,)),
-            pltpu.SemaphoreType.DMA((2,)),
+            pltpu.SemaphoreType.DMA((4,)),
             pltpu.SemaphoreType.DMA((GROUPS,)),
             pltpu.SemaphoreType.DMA((GROUPS,)),
             pltpu.SemaphoreType.DMA((3,)),
@@ -316,18 +325,26 @@
 
 
 def finish_kernel(
-    done_hbm, last_hbm, o_hbm, received, rows, scale_col, scale_row, staged, sems, copy_sems
+    done_hbm, last_hbm, o_hbm, received, rows, scale_col, scale_row, staged, passing, sems, copy_sems
 ):
     load = pltpu.make_async_copy(last_hbm, received, sems.at[0])
     load.start()
-    copies = [
-        pltpu.make_async_copy(done_hbm.at[c, p], o_hbm.at[c, p], copy_sems.at[c, p])
+    ins = [
+        pltpu.make_async_copy(done_hbm.at[c, p], passing.at[c, p], copy_sems.at[0, c, p])
         for c in range(3)
         for p in range(2)
     ]
-    for copy in copies:
+    copies = [
+        pltpu.make_async_copy(passing.at[c, p], o_hbm.at[c, p], copy_sems.at[1, c, p])
+        for c in range(3)
+        for p in range(2)
+    ]
+    for copy in ins:
         copy.start()
     load.wait()
+    for n, copy in enumerate(copies):
+        ins[n].wait()
+        copy.start()
     correlate_channel(received, rows, scale_col, scale_row, staged)
     store = pltpu.make_async_copy(staged, o_hbm.at[3], sems.at[1])
     store.start()
@@ -348,8 +365,9 @@
             pltpu.VMEM((INPUTS, 128), jnp.float32),
             pltpu.VMEM((1, INPUTS), jnp.float32),
             pltpu.VMEM((2, INPUTS, INPUTS), jnp.bfloat16),
+            pltpu.VMEM((3, 2, INPUTS, INPUTS), jnp.bfloat16),
             pltpu.SemaphoreType.DMA((2,)),
-            pltpu.SemaphoreType.DMA((3, 2)),
+            pltpu.SemaphoreType.DMA((2, 3, 2)),
         ],
         compiler_params=pltpu.CompilerParams(vmem_limit_bytes=60 * 1024 * 1024),
         name="finish",

time: 525 us -> 131 us (0.25)
  Pallas kernels: 524 us -> 130 us
    pallas_call x1, Pallas kernels: 382 us -> 11.9 us  [finish(): pl.pallas_call(finish_kernel, out_shape=jax.ShapeDtypeStruct((GROUPS, 2,...]
    pallas_call x1, Pallas kernels: 141 us -> 118 us  [channelize(): pl.pallas_call(channelize_kernel, out_shape=(jax.ShapeDtypeStruct((3, 2,...]
where the time goes in v3:
time: 131 us; the launch traced here: 130 us
  Pallas kernels  130 us (99%)
    pallas_call x1, Pallas kernels, channelize(): pl.pallas_call(channelize_kernel, out_shape=(jax.ShapeDtypeStruct((3, 2,...  118 us
    pallas_call x1, Pallas kernels, finish(): pl.pallas_call(finish_kernel, out_shape=jax.ShapeDtypeStruct((GROUPS, 2,...  11.9 us

profile of v3, /device:TPU:1, one launch (start us, length us, event | category | flops | bytes accessed | tf_op | source)
XLA Modules:
  0.0 129.7 jit_solution(9047516292426126269)
XLA Ops:
  0.0 117.8 %channelize.1 = (bf16[3,2,1024,1024]{3,2,1,0:T(8,128)(2,1)}, bf16[16,8,2,2,16,128]{5,4,3,2,1,0:T(8,128)(2,1)}) custom-call(bf16[64,65536]{1,0:T(8,128)(2,1)} %v_hbm.1, f32[8,1024]{1,0:T(8,128)} %proto_ref.1, bf16[4,256,1024]{2,1,0:T(8,128)(2,1)} %constant.2.clone.table_hbm), custom_call_target="tpu_custom_call" | custom-call | tf_op jit(solution)/shard_map/channelize/pallas_call | solution.py:289
  117.8 11.9 %finish.1 = bf16[4,2,1024,1024]{3,2,1,0:T(8,128)(2,1)} custom-call(bf16[3,2,1024,1024]{3,2,1,0:T(8,128)(2,1)} %get-tuple-element.7.done_hbm, bf16[16,8,2,2,16,128]{5,4,3,2,1,0:T(8,128)(2,1)} %get-tuple-element.8.last_hbm), custom_call_target="tpu_custom_call" | custom-call | tf_op jit(solution)/shard_map/finish/pallas_call | solution.py:357

commit v4 on v3

--- a/solution.py
+++ b/solution.py
@@ -91,9 +91,9 @@
 
 
 def channelize_kernel(
-    v_hbm, proto_ref, table_hbm, done_hbm, last_hbm,
-    v, table, filtered, turned, outbox, inbox, rows, scale_col, scale_row, staged,
-    v_sems, table_sem, own_sems, halo_sems, send_sems, recv_sems, done_sems,
+    v_hbm, proto_ref, table_hbm, done, last,
+    v, table, filtered, turned, outbox, inbox, rows, scale_col, scale_row,
+    v_sems, table_sem, own_sems, halo_sems, send_sems, recv_sems,
 ):
     a = lax.axis_index("inp")
     b = lax.axis_index("tm")
@@ -235,11 +235,11 @@
 
         @pl.when(j == 3)
         def _():
-            send(3, lambda other: outbox.at[3, other], last_hbm.at[a, b])
+            send(3, lambda other: outbox.at[3, other], last.at[a, b])
 
     owns = [
         pltpu.make_async_copy(
-            outbox.at[j, me], inbox.at[j, a, b] if j < 3 else last_hbm.at[a, b], own_sems.at[j]
+            outbox.at[j, me], inbox.at[j, a, b] if j < 3 else last.at[a, b], own_sems.at[j]
         )
         for j in range(GROUPS)
     ]
@@ -256,9 +256,6 @@
         some = outbox.at[j, pl.ds(0, DEVICES - 1)]
         pltpu.make_async_copy(some, some, recv_sems.at[j]).wait()
 
-    def written(j):
-        return pltpu.make_async_copy(staged.at[lax.rem(j, 2)], done_hbm.at[j], done_sems.at[j])
-
     for j in range(3):
         owns[j].wait()
 
@@ -266,15 +263,8 @@
     def _(j):
         arrived(j)
 
-        @pl.when(j == 2)
-        def _():
-            written(0).wait()
-
-        correlate_channel(inbox.at[j], rows, scale_col, scale_row, staged.at[lax.rem(j, 2)])
-        written(j).start()
-
-    written(1).wait()
-    written(2).wait()
+        correlate_channel(inbox.at[j], rows, scale_col, scale_row, done.at[j])
+
     owns[3].wait()
     arrived(3)
 
@@ -289,15 +279,15 @@
     return pl.pallas_call(
         channelize_kernel,
         out_shape=(
-            jax.ShapeDtypeStruct((3, 2, INPUTS, INPUTS), jnp.bfloat16),
-            jax.ShapeDtypeStruct(piece, jnp.bfloat16),
+            pltpu.VMEM((3, 2, INPUTS, INPUTS), jnp.bfloat16),
+            pltpu.VMEM(piece, jnp.bfloat16),
         ),
         in_specs=[
             pl.BlockSpec(memory_space=pl.ANY),
             pl.BlockSpec(memory_space=pltpu.VMEM),
             pl.BlockSpec(memory_space=pl.ANY),
         ],
-        out_specs=(pl.BlockSpec(memory_space=pl.ANY), pl.BlockSpec(memory_space=pl.ANY)),
+        out_specs=(pl.BlockSpec(memory_space=pltpu.VMEM), pl.BlockSpec(memory_space=pltpu.VMEM)),
         scratch_shapes=[
             pltpu.VMEM((INPUTS_DEV, (SPEC_DEV + HALO) * FRAME), jnp.bfloat16),
             pltpu.VMEM((GROUPS, 2 * DEVICES, FRAME), jnp.bfloat16),
@@ -308,68 +298,45 @@
             pltpu.VMEM((INPUTS, INPUTS), jnp.bfloat16),
             pltpu.VMEM((INPUTS, 128), jnp.float32),
             pltpu.VMEM((1, INPUTS), jnp.float32),
-            pltpu.VMEM((2, 2, INPUTS, INPUTS), jnp.bfloat16),
             pltpu.SemaphoreType.DMA((4,)),
             pltpu.SemaphoreType.DMA,
             pltpu.SemaphoreType.DMA((GROUPS,)),
             pltpu.SemaphoreType.DMA((4,)),
             pltpu.SemaphoreType.DMA((GROUPS,)),
             pltpu.SemaphoreType.DMA((GROUPS,)),
-            pltpu.SemaphoreType.DMA((3,)),
         ],
         compiler_params=pltpu.CompilerParams(
-            collective_id=0, has_side_effects=True, vmem_limit_bytes=60 * 1024 * 1024
+            collective_id=0, has_side_effects=True, vmem_limit_bytes=42 * 1024 * 1024
         ),
         name="channelize",
     )(voltages, prototype, table)
 
 
-def finish_kernel(
-    done_hbm, last_hbm, o_hbm, received, rows, scale_col, scale_row, staged, passing, sems, copy_sems
-):
-    load = pltpu.make_async_copy(last_hbm, received, sems.at[0])
-    load.start()
-    ins = [
-        pltpu.make_async_copy(done_hbm.at[c, p], passing.at[c, p], copy_sems.at[0, c, p])
-        for c in range(3)
-        for p in range(2)
-    ]
-    copies = [
-        pltpu.make_async_copy(passing.at[c, p], o_hbm.at[c, p], copy_sems.at[1, c, p])
-        for c in range(3)
-        for p in range(2)
-    ]
-    for copy in ins:
+def finish_kernel(done, last, o_hbm, rows, scale_col, scale_row, staged, sems):
+    copies = [pltpu.make_async_copy(done.at[c], o_hbm.at[c], sems.at[c]) for c in range(3)]
+    for copy in copies:
         copy.start()
-    load.wait()
-    for n, copy in enumerate(copies):
-        ins[n].wait()
-        copy.start()
-    correlate_channel(received, rows, scale_col, scale_row, staged)
-    store = pltpu.make_async_copy(staged, o_hbm.at[3], sems.at[1])
-    store.start()
+    correlate_channel(last, rows, scale_col, scale_row, staged)
+    copies.append(pltpu.make_async_copy(staged, o_hbm.at[3], sems.at[3]))
+    copies[3].start()
     for copy in copies:
         copy.wait()
-    store.wait()
 
 
 def finish(done, last):
     return pl.pallas_call(
         finish_kernel,
         out_shape=jax.ShapeDtypeStruct((GROUPS, 2, INPUTS, INPUTS), jnp.bfloat16),
-        in_specs=[pl.BlockSpec(memory_space=pl.ANY)] * 2,
+        in_specs=[pl.BlockSpec(memory_space=pltpu.VMEM)] * 2,
         out_specs=pl.BlockSpec(memory_space=pl.ANY),
         scratch_shapes=[
-            pltpu.VMEM((INP, TM, 2, 2, PAIRS, 128), jnp.bfloat16),
             pltpu.VMEM((INPUTS, INPUTS), jnp.bfloat16),
             pltpu.VMEM((INPUTS, 128), jnp.float32),
             pltpu.VMEM((1, INPUTS), jnp.float32),
             pltpu.VMEM((2, INPUTS, INPUTS), jnp.bfloat16),
-            pltpu.VMEM((3, 2, INPUTS, INPUTS), jnp.bfloat16),
-            pltpu.SemaphoreType.DMA((2,)),
-            pltpu.SemaphoreType.DMA((2, 3, 2)),
+            pltpu.SemaphoreType.DMA((GROUPS,)),
         ],
-        compiler_params=pltpu.CompilerParams(vmem_limit_bytes=60 * 1024 * 1024),
+        compiler_params=pltpu.CompilerParams(vmem_limit_bytes=20 * 1024 * 1024),
         name="finish",
     )(done, last)
 

time: 131 us -> 124 us (0.947); the launches traced: 130 us -> 124 us
  Pallas kernels: 130 us -> 124 us
    pallas_call x1, Pallas kernels: 11.9 us -> 6.54 us  [finish(): pl.pallas_call(finish_kernel, out_shape=jax.ShapeDtypeStruct((GROUPS, 2,...]
where the time goes in v4:
time: 124 us
  Pallas kernels  124 us (100%)
    pallas_call x1, Pallas kernels, channelize(): pl.pallas_call(channelize_kernel, out_shape=(pltpu.VMEM((3, 2, INPUTS, IN...  118 us
    pallas_call x1, Pallas kernels, finish(): pl.pallas_call(finish_kernel, out_shape=jax.ShapeDtypeStruct((GROUPS, 2,...  6.54 us

profile of v4, /device:TPU:1, one launch (start us, length us, event | category | flops | bytes accessed | tf_op | source)
XLA Modules:
  0.0 124.2 jit_solution(9024952436265949237)
XLA Ops:
  0.0 117.7 %channelize.1 = (bf16[3,2,1024,1024]{3,2,1,0:T(8,128)(2,1)S(1)}, bf16[16,8,2,2,16,128]{5,4,3,2,1,0:T(8,128)(2,1)S(1)}) custom-call(bf16[64,65536]{1,0:T(8,128)(2,1)} %v_hbm.1, f32[8,1024]{1,0:T(8,128)} %proto_ref.1, bf16[4,256,1024]{2,1,0:T(8,128)(2,1)} %constant.2.clone.table_hbm), custom_call_target="tpu_custom_call" | custom-call | tf_op jit(solution)/shard_map/channelize/pallas_call | solution.py:279
  117.7 6.5 %finish.1 = bf16[4,2,1024,1024]{3,2,1,0:T(8,128)(2,1)} custom-call(bf16[3,2,1024,1024]{3,2,1,0:T(8,128)(2,1)S(1)} %get-tuple-element.7.done, bf16[16,8,2,2,16,128]{5,4,3,2,1,0:T(8,128)(2,1)S(1)} %get-tuple-element.8.last), custom_call_target="tpu_custom_call" | custom-call | tf_op jit(solution)/shard_map/finish/pallas_call | solution.py:327

commit v5 on v4

--- a/solution.py
+++ b/solution.py
@@ -21,8 +21,9 @@
 GROUPS = 4
 INP = 16
 TM = 8
-HALF = SPEC_DEV // 2
-PAIRS = HALF // 2
+QUARTERS = 4
+QUARTER = SPEC_DEV // QUARTERS
+PAIRS = QUARTER // 2
 STRIDE = PAIRS + 1
 TILE = 256
 MESH = pl.DeviceIdType.MESH
@@ -36,36 +37,38 @@
     return table.reshape(GROUPS, 2 * DEVICES, FRAME).astype(jnp.bfloat16)
 
 
-def correlate_channel(received, rows, scale_col, scale_row, out):
+def correlate_channel(received, rows, swapped, scale_col, scale_row, out, finished=None):
+    half = INPUTS // 2
+
     @pl.loop(0, INP)
     def _(a):
         at = pl.ds(pl.multiple_of(a * INPUTS_DEV, INPUTS_DEV), INPUTS_DEV)
-        for p in range(2):
-            turned = received[a, :, :, p].reshape(TM * HALF, 128).T
-            for h in range(2):
-                base = (2 * p + h) * TM * HALF
-                rows[at, base : base + TM * HALF] = turned[h * 64 : (h + 1) * 64]
-
-    half = INPUTS // 2
-
-    def grams(left, right, n):
+        turned = received[a].reshape(half, 128).T
+        for h in range(2):
+            rows[at, h * half : (h + 1) * half] = turned[h * 64 : (h + 1) * 64]
+
+    def grams(m, n):
         other = rows[n * TILE : (n + 1) * TILE, :]
         dims = (((1,), (1,)), ((), ()))
-        return (
-            lax.dot_general(left, other, dims, preferred_element_type=jnp.float32),
-            lax.dot_general(right, other, dims, preferred_element_type=jnp.float32),
-        )
-
-    def sides(m):
-        left = rows[m * TILE : (m + 1) * TILE, :]
-        return left, jnp.concatenate([left[:, half:], -left[:, :half]], axis=1)
-
+        return [
+            lax.dot_general(
+                ref[m * TILE : (m + 1) * TILE, :], other, dims, preferred_element_type=jnp.float32
+            )
+            for ref in (rows, swapped)
+        ]
+
+    first = lax.rem(lax.broadcasted_iota(jnp.int32, (TILE, 128), 1), 2 * PAIRS) < PAIRS
     eye = lax.broadcasted_iota(jnp.int32, (TILE, TILE), 0) == lax.broadcasted_iota(
         jnp.int32, (TILE, TILE), 1
     )
     for m in range(INPUTS // TILE):
         at = slice(m * TILE, (m + 1) * TILE)
-        real, imag = grams(*sides(m), m)
+        for n in range(INPUTS // 128):
+            to = slice(n * 128, (n + 1) * 128)
+            some = rows[at, to]
+            ahead = pltpu.roll(some, 128 - PAIRS, 1)
+            swapped[at, to] = jnp.where(first, ahead, -pltpu.roll(some, PAIRS, 1))
+        real, imag = grams(m, m)
         diagonal = jnp.where(eye, real, 0.0)
         column = lax.rsqrt(jnp.sum(diagonal, axis=1, keepdims=True) + 1e-06)
         row = lax.rsqrt(jnp.sum(diagonal, axis=0, keepdims=True) + 1e-06)
@@ -75,24 +78,25 @@
         out[0, at, at] = (real * outer).astype(jnp.bfloat16)
         out[1, at, at] = (imag * outer).astype(jnp.bfloat16)
     for m in range(INPUTS // TILE - 1):
-        left, right = sides(m)
         at = slice(m * TILE, (m + 1) * TILE)
         column = scale_col[at, 0:1]
         for n in range(m + 1, INPUTS // TILE):
             to = slice(n * TILE, (n + 1) * TILE)
             outer = column * scale_row[:, to]
-            real, imag = grams(left, right, n)
+            real, imag = grams(m, n)
             real = (real * outer).astype(jnp.bfloat16)
             imag = (imag * outer).astype(jnp.bfloat16)
             out[0, at, to] = real
             out[1, at, to] = imag
             out[0, to, at] = real.T
             out[1, to, at] = -imag.T
+        if finished is not None:
+            finished(m)
 
 
 def channelize_kernel(
     v_hbm, proto_ref, table_hbm, done, last,
-    v, table, filtered, turned, outbox, inbox, rows, scale_col, scale_row,
+    v, table, filtered, turned, outbox, inbox, rows, swapped, scale_col, scale_row,
     v_sems, table_sem, own_sems, halo_sems, send_sems, recv_sems,
 ):
     a = lax.axis_index("inp")
@@ -105,11 +109,9 @@
 
     loads = [
         pltpu.make_async_copy(
-            v_hbm.at[pl.ds(q * 16, 16), :],
-            v.at[pl.ds(q * 16, 16), frames(BEFORE, SPEC_DEV)],
-            v_sems.at[q],
-        )
-        for q in range(4)
+            v_hbm.at[:, frames(first, count)], v.at[:, frames(BEFORE + first, count)], v_sems.at[n]
+        )
+        for n, (first, count) in enumerate(((12, 23), (35, 29), (0, 12)))
     ]
     for load in loads:
         load.start()
@@ -146,17 +148,16 @@
                     total = total + taps[k] * x[s + k]
                 filtered[slot + s, at, lanes] = total.astype(jnp.bfloat16)
 
-    def dft(j, half):
-        block = filtered[pl.ds(half * HALF, HALF)].reshape(HALF * INPUTS_DEV, FRAME)
+    def dft(j, quarter):
+        block = filtered[pl.ds(quarter * QUARTER, QUARTER)].reshape(QUARTER * INPUTS_DEV, FRAME)
         out = lax.dot_general(
             table[j], block, (((1,), (1,)), ((), ())), preferred_element_type=jnp.float32
         )
         for l in range(PAIRS):
             turned[pl.ds(l, 2 * DEVICES, stride=STRIDE), :] = out[:, l * 128 : (l + 1) * 128]
-        for m in range(2 * DEVICES):
-            outbox[j, m // 2, half, m % 2] = turned[pl.ds(m * STRIDE, PAIRS), :].astype(
-                jnp.bfloat16
-            )
+        for d in range(DEVICES):
+            parts = [turned[pl.ds((2 * d + p) * STRIDE, PAIRS), :] for p in range(2)]
+            outbox[j, d, quarter] = jnp.concatenate(parts, axis=0).astype(jnp.bfloat16)
 
     def send(j, source, target):
         @pl.loop(1, DEVICES)
@@ -183,8 +184,10 @@
 
     forward = halo(SPEC_DEV, BEFORE, 0, 1, 0)
     back = halo(BEFORE, AFTER, BEFORE + SPEC_DEV, TM - 1, 1)
-    for load in loads:
-        load.wait()
+    loads[0].wait()
+    pl.loop(0, 4)(lambda q: fir(2, q))
+    loads[1].wait()
+    loads[2].wait()
     pl.semaphore_wait(barrier, DEVICES - 1)
     back.start()
 
@@ -192,13 +195,22 @@
     def _():
         forward.start()
 
-    pl.loop(0, 16)(lambda t: fir(2 + lax.div(t, 4), lax.rem(t, 4)))
+    pl.loop(0, 4)(lambda q: fir(3, q))
     table_load.wait()
 
     @pl.loop(0, 2)
-    def _(j):
-        dft(j, 0)
-        send(j, lambda other: outbox.at[j, other, 0], inbox.at[j, a, b, 0])
+    def _(quarter):
+        @pl.when(quarter == 1)
+        def _():
+            pl.loop(0, 8)(lambda t: fir(4 + lax.div(t, 4), lax.rem(t, 4)))
+
+        dft(0, quarter)
+        send(0, lambda other: outbox.at[0, other, quarter], inbox.at[0, a, b, quarter])
+
+    low = pl.ds(0, 2)
+    high = pl.ds(2, 2)
+    pl.loop(0, 2)(lambda quarter: dft(1, quarter))
+    send(1, lambda other: outbox.at[1, other, low], inbox.at[1, a, b, low])
 
     pl.loop(0, 8)(lambda t: fir(6 - 5 * lax.div(t, 4), lax.rem(t, 4)))
 
@@ -220,14 +232,12 @@
 
     @pl.loop(0, 2)
     def _(j):
-        dft(j, 1)
-        send(j, lambda other: outbox.at[j, other, 1], inbox.at[j, a, b, 1])
+        pl.loop(2, 4)(lambda quarter: dft(j, quarter))
+        send(j, lambda other: outbox.at[j, other, high], inbox.at[j, a, b, high])
 
     @pl.loop(2, GROUPS)
     def _(j):
-        @pl.loop(0, 2)
-        def _(half):
-            dft(j, half)
+        pl.loop(0, QUARTERS)(lambda quarter: dft(j, quarter))
 
         @pl.when(j == 2)
         def _():
@@ -263,7 +273,7 @@
     def _(j):
         arrived(j)
 
-        correlate_channel(inbox.at[j], rows, scale_col, scale_row, done.at[j])
+        correlate_channel(inbox.at[j], rows, swapped, scale_col, scale_row, done.at[j])
 
     owns[3].wait()
     arrived(3)
@@ -275,7 +285,7 @@
 
 
 def channelize(voltages, prototype, table):
-    piece = (INP, TM, 2, 2, PAIRS, 128)
+    piece = (INP, TM, QUARTERS, 2 * PAIRS, 128)
     return pl.pallas_call(
         channelize_kernel,
         out_shape=(
@@ -293,12 +303,13 @@
             pltpu.VMEM((GROUPS, 2 * DEVICES, FRAME), jnp.bfloat16),
             pltpu.VMEM((SPEC_DEV, INPUTS_DEV, FRAME), jnp.bfloat16),
             pltpu.VMEM((2 * DEVICES * STRIDE, 128), jnp.float32),
-            pltpu.VMEM((GROUPS, DEVICES, 2, 2, PAIRS, 128), jnp.bfloat16),
+            pltpu.VMEM((GROUPS, DEVICES, QUARTERS, 2 * PAIRS, 128), jnp.bfloat16),
             pltpu.VMEM((3, *piece), jnp.bfloat16),
+            pltpu.VMEM((INPUTS, INPUTS), jnp.bfloat16),
             pltpu.VMEM((INPUTS, INPUTS), jnp.bfloat16),
             pltpu.VMEM((INPUTS, 128), jnp.float32),
             pltpu.VMEM((1, INPUTS), jnp.float32),
-            pltpu.SemaphoreType.DMA((4,)),
+            pltpu.SemaphoreType.DMA((3,)),
             pltpu.SemaphoreType.DMA,
             pltpu.SemaphoreType.DMA((GROUPS,)),
             pltpu.SemaphoreType.DMA((4,)),
@@ -306,19 +317,25 @@
             pltpu.SemaphoreType.DMA((GROUPS,)),
         ],
         compiler_params=pltpu.CompilerParams(
-            collective_id=0, has_side_effects=True, vmem_limit_bytes=42 * 1024 * 1024
+            collective_id=0, has_side_effects=True, vmem_limit_bytes=43 * 1024 * 1024
         ),
         name="channelize",
     )(voltages, prototype, table)
 
 
-def finish_kernel(done, last, o_hbm, rows, scale_col, scale_row, staged, sems):
+def finish_kernel(done, last, o_hbm, rows, swapped, scale_col, scale_row, staged, sems):
     copies = [pltpu.make_async_copy(done.at[c], o_hbm.at[c], sems.at[c]) for c in range(3)]
     for copy in copies:
         copy.start()
-    correlate_channel(last, rows, scale_col, scale_row, staged)
-    copies.append(pltpu.make_async_copy(staged, o_hbm.at[3], sems.at[3]))
-    copies[3].start()
+
+    def finished(m):
+        at = pl.ds(m * TILE, TILE if m < 2 else 2 * TILE)
+        copies.append(
+            pltpu.make_async_copy(staged.at[:, at], o_hbm.at[3, :, at], sems.at[3 + m])
+        )
+        copies[-1].start()
+
+    correlate_channel(last, rows, swapped, scale_col, scale_row, staged, finished)
     for copy in copies:
         copy.wait()
 
@@ -331,10 +348,11 @@
         out_specs=pl.BlockSpec(memory_space=pl.ANY),
         scratch_shapes=[
             pltpu.VMEM((INPUTS, INPUTS), jnp.bfloat16),
+            pltpu.VMEM((INPUTS, INPUTS), jnp.bfloat16),
             pltpu.VMEM((INPUTS, 128), jnp.float32),
             pltpu.VMEM((1, INPUTS), jnp.float32),
             pltpu.VMEM((2, INPUTS, INPUTS), jnp.bfloat16),
-            pltpu.SemaphoreType.DMA((GROUPS,)),
+            pltpu.SemaphoreType.DMA((6,)),
         ],
         compiler_params=pltpu.CompilerParams(vmem_limit_bytes=20 * 1024 * 1024),
         name="finish",

time: 124 us -> 124 us (level)
  no operation moved by 1% of the time
where the time goes in v5:
time: 124 us
  Pallas kernels  124 us (100%)
    pallas_call x1, Pallas kernels, channelize(): pl.pallas_call(channelize_kernel, out_shape=(pltpu.VMEM((3, 2, INPUTS, IN...  118 us
    pallas_call x1, Pallas kernels, finish(): pl.pallas_call(finish_kernel, out_shape=jax.ShapeDtypeStruct((GROUPS, 2,...  6.43 us

profile of v5, /device:TPU:1, one launch (start us, length us, event | category | flops | bytes accessed | tf_op | source)
XLA Modules:
  0.0 124.0 jit_solution(5545051472315963178)
XLA Ops:
  0.0 117.5 %channelize.1 = (bf16[3,2,1024,1024]{3,2,1,0:T(8,128)(2,1)S(1)}, bf16[16,8,4,16,128]{4,3,2,1,0:T(8,128)(2,1)S(1)}) custom-call(bf16[64,65536]{1,0:T(8,128)(2,1)} %v_hbm.1, f32[8,1024]{1,0:T(8,128)} %proto_ref.1, bf16[4,256,1024]{2,1,0:T(8,128)(2,1)} %constant.2.clone.table_hbm), custom_call_target="tpu_custom_call" | custom-call | tf_op jit(solution)/shard_map/channelize/pallas_call | solution.py:289
  117.6 6.4 %finish.1 = bf16[4,2,1024,1024]{3,2,1,0:T(8,128)(2,1)} custom-call(bf16[3,2,1024,1024]{3,2,1,0:T(8,128)(2,1)S(1)} %get-tuple-element.7.done, bf16[16,8,4,16,128]{4,3,2,1,0:T(8,128)(2,1)S(1)} %get-tuple-element.8.last), custom_call_target="tpu_custom_call" | custom-call | tf_op jit(solution)/shard_map/finish/pallas_call | solution.py:344

commit v6 on v5

--- a/solution.py
+++ b/solution.py
@@ -97,7 +97,7 @@
 def channelize_kernel(
     v_hbm, proto_ref, table_hbm, done, last,
     v, table, filtered, turned, outbox, inbox, rows, swapped, scale_col, scale_row,
-    v_sems, table_sem, own_sems, halo_sems, send_sems, recv_sems,
+    v_sems, table_sem, own_sems, halo_sems, send_sems, recv_sems, row_sem,
 ):
     a = lax.axis_index("inp")
     b = lax.axis_index("tm")
@@ -105,13 +105,13 @@
     barrier = pltpu.get_barrier_semaphore()
 
     def frames(first, count):
-        return pl.ds(first * FRAME, count * FRAME)
+        return pl.ds(pl.multiple_of(first * FRAME, FRAME), count * FRAME)
 
     loads = [
         pltpu.make_async_copy(
             v_hbm.at[:, frames(first, count)], v.at[:, frames(BEFORE + first, count)], v_sems.at[n]
         )
-        for n, (first, count) in enumerate(((12, 23), (35, 29), (0, 12)))
+        for n, (first, count) in enumerate(((12, 24), (36, 28), (0, 12)))
     ]
     for load in loads:
         load.start()
@@ -122,10 +122,20 @@
         other = lax.rem(me + k * 37, DEVICES)
         return other, {"inp": lax.div(other, TM), "tm": lax.rem(other, TM)}
 
-    @pl.loop(1, DEVICES)
+    @pl.loop(1, INP)
     def _(k):
-        _, where = place(k)
-        pl.semaphore_signal(barrier, inc=1, device_id=where, device_id_type=MESH)
+        pl.semaphore_signal(
+            barrier, inc=1, device_id={"inp": lax.rem(a + k, INP)}, device_id_type=MESH
+        )
+
+    def signal_row(semaphore):
+        @pl.loop(1, TM)
+        def _(k):
+            pl.semaphore_signal(
+                semaphore, inc=1, device_id={"tm": lax.rem(b + k, TM)}, device_id_type=MESH
+            )
+
+    signal_row(barrier)
 
     def fir(chunk, q, last=False):
         at = pl.ds(pl.multiple_of(q * 16, 16), 16)
@@ -188,15 +198,18 @@
     pl.loop(0, 4)(lambda q: fir(2, q))
     loads[1].wait()
     loads[2].wait()
-    pl.semaphore_wait(barrier, DEVICES - 1)
+    pl.semaphore_wait(barrier, INP + TM - 2)
     back.start()
 
     @pl.when(b < TM - 1)
     def _():
         forward.start()
 
+    signal_row(row_sem)
+
     pl.loop(0, 4)(lambda q: fir(3, q))
     table_load.wait()
+    pl.semaphore_wait(row_sem, TM - 1)
 
     @pl.loop(0, 2)
     def _(quarter):
@@ -315,6 +328,7 @@
             pltpu.SemaphoreType.DMA((4,)),
             pltpu.SemaphoreType.DMA((GROUPS,)),
             pltpu.SemaphoreType.DMA((GROUPS,)),
+            pltpu.SemaphoreType.REGULAR,
         ],
         compiler_params=pltpu.CompilerParams(
             collective_id=0, has_side_effects=True, vmem_limit_bytes=43 * 1024 * 1024

time: 124 us -> 122 us (0.984)
  Pallas kernels: 124 us -> 122 us
    pallas_call x1, Pallas kernels: 118 us -> 115 us  [channelize(): pl.pallas_call(channelize_kernel, out_shape=(pltpu.VMEM((3, 2, INPUTS, IN...]
where the time goes in v6:
time: 122 us
  Pallas kernels  122 us (100%)
    pallas_call x1, Pallas kernels, channelize(): pl.pallas_call(channelize_kernel, out_shape=(pltpu.VMEM((3, 2, INPUTS, IN...  115 us
    pallas_call x1, Pallas kernels, finish(): pl.pallas_call(finish_kernel, out_shape=jax.ShapeDtypeStruct((GROUPS, 2,...  6.43 us

profile of v6, /device:TPU:1, one launch (start us, length us, event | category | flops | bytes accessed | tf_op | source)
XLA Modules:
  0.0 121.8 jit_solution(7763107700342470699)
XLA Ops:
  0.0 115.4 %channelize.1 = (bf16[3,2,1024,1024]{3,2,1,0:T(8,128)(2,1)S(1)}, bf16[16,8,4,16,128]{4,3,2,1,0:T(8,128)(2,1)S(1)}) custom-call(bf16[64,65536]{1,0:T(8,128)(2,1)} %v_hbm.1, f32[8,1024]{1,0:T(8,128)} %proto_ref.1, bf16[4,256,1024]{2,1,0:T(8,128)(2,1)} %constant.2.clone.table_hbm), custom_call_target="tpu_custom_call" | custom-call | tf_op jit(solution)/shard_map/channelize/pallas_call | solution.py:302
  115.4 6.4 %finish.1 = bf16[4,2,1024,1024]{3,2,1,0:T(8,128)(2,1)} custom-call(bf16[3,2,1024,1024]{3,2,1,0:T(8,128)(2,1)S(1)} %get-tuple-element.7.done, bf16[16,8,4,16,128]{4,3,2,1,0:T(8,128)(2,1)S(1)} %get-tuple-element.8.last), custom_call_target="tpu_custom_call" | custom-call | tf_op jit(solution)/shard_map/finish/pallas_call | solution.py:358

commit v7 on v6

--- a/solution.py
+++ b/solution.py
@@ -26,6 +26,7 @@
 PAIRS = QUARTER // 2
 STRIDE = PAIRS + 1
 TILE = 256
+TILES = [(m, n) for m in range(INPUTS // TILE) for n in range(m, INPUTS // TILE)]
 MESH = pl.DeviceIdType.MESH
 
 
@@ -37,25 +38,39 @@
     return table.reshape(GROUPS, 2 * DEVICES, FRAME).astype(jnp.bfloat16)
 
 
-def correlate_channel(received, rows, swapped, scale_col, scale_row, out, finished=None):
-    half = INPUTS // 2
+def correlate_channel(
+    parts, rows, swapped, scale_col, scale_row, out, held=None, finished=None
+):
+    depth = INPUTS // 4
+    width = 2 * depth * len(parts)
 
     @pl.loop(0, INP)
     def _(a):
         at = pl.ds(pl.multiple_of(a * INPUTS_DEV, INPUTS_DEV), INPUTS_DEV)
-        turned = received[a].reshape(half, 128).T
-        for h in range(2):
-            rows[at, h * half : (h + 1) * half] = turned[h * 64 : (h + 1) * 64]
+        for n, part in enumerate(parts):
+            turned = part[a].reshape(depth, 128).T
+            for h in range(2):
+                base = (2 * n + h) * depth
+                rows[at, base : base + depth] = turned[h * 64 : (h + 1) * 64]
 
     def grams(m, n):
-        other = rows[n * TILE : (n + 1) * TILE, :]
+        other = rows[n * TILE : (n + 1) * TILE, :width]
         dims = (((1,), (1,)), ((), ()))
-        return [
+        pair = [
             lax.dot_general(
-                ref[m * TILE : (m + 1) * TILE, :], other, dims, preferred_element_type=jnp.float32
+                ref[m * TILE : (m + 1) * TILE, :width],
+                other,
+                dims,
+                preferred_element_type=jnp.float32,
             )
             for ref in (rows, swapped)
         ]
+        if out is None:
+            for k in range(2):
+                held[TILES.index((m, n)), k] = pair[k]
+        elif held is not None:
+            pair = [pair[k] + held[TILES.index((m, n)), k] for k in range(2)]
+        return pair
 
     first = lax.rem(lax.broadcasted_iota(jnp.int32, (TILE, 128), 1), 2 * PAIRS) < PAIRS
     eye = lax.broadcasted_iota(jnp.int32, (TILE, TILE), 0) == lax.broadcasted_iota(
@@ -63,11 +78,13 @@
     )
     for m in range(INPUTS // TILE):
         at = slice(m * TILE, (m + 1) * TILE)
-        for n in range(INPUTS // 128):
+        for n in range(width // 128):
             to = slice(n * 128, (n + 1) * 128)
             some = rows[at, to]
             ahead = pltpu.roll(some, 128 - PAIRS, 1)
             swapped[at, to] = jnp.where(first, ahead, -pltpu.roll(some, PAIRS, 1))
+        if out is None:
+            continue
         real, imag = grams(m, m)
         diagonal = jnp.where(eye, real, 0.0)
         column = lax.rsqrt(jnp.sum(diagonal, axis=1, keepdims=True) + 1e-06)
@@ -77,6 +94,10 @@
         outer = column * row
         out[0, at, at] = (real * outer).astype(jnp.bfloat16)
         out[1, at, at] = (imag * outer).astype(jnp.bfloat16)
+    if out is None:
+        for m, n in TILES:
+            grams(m, n)
+        return
     for m in range(INPUTS // TILE - 1):
         at = slice(m * TILE, (m + 1) * TILE)
         column = scale_col[at, 0:1]
@@ -95,8 +116,8 @@
 
 
 def channelize_kernel(
-    v_hbm, proto_ref, table_hbm, done, last,
-    v, table, filtered, turned, outbox, inbox, rows, swapped, scale_col, scale_row,
+    v_hbm, proto_ref, table_hbm, done, held, last,
+    v, table, filtered, turned, outbox, inbox, early, rows, swapped, scale_col, scale_row,
     v_sems, table_sem, own_sems, halo_sems, send_sems, recv_sems, row_sem,
 ):
     a = lax.axis_index("inp")
@@ -169,7 +190,7 @@
             parts = [turned[pl.ds((2 * d + p) * STRIDE, PAIRS), :] for p in range(2)]
             outbox[j, d, quarter] = jnp.concatenate(parts, axis=0).astype(jnp.bfloat16)
 
-    def send(j, source, target):
+    def send(j, source, target, arrival=None):
         @pl.loop(1, DEVICES)
         def _(k):
             other, where = place(k)
@@ -177,7 +198,7 @@
                 src_ref=source(other),
                 dst_ref=target,
                 send_sem=send_sems.at[j],
-                recv_sem=recv_sems.at[j],
+                recv_sem=recv_sems.at[j if arrival is None else arrival],
                 device_id=where,
                 device_id_type=MESH,
             ).start()
@@ -248,23 +269,27 @@
         pl.loop(2, 4)(lambda quarter: dft(j, quarter))
         send(j, lambda other: outbox.at[j, other, high], inbox.at[j, a, b, high])
 
-    @pl.loop(2, GROUPS)
-    def _(j):
-        pl.loop(0, QUARTERS)(lambda quarter: dft(j, quarter))
-
-        @pl.when(j == 2)
+    pl.loop(0, QUARTERS)(lambda quarter: dft(2, quarter))
+    send(2, lambda other: outbox.at[2, other], inbox.at[2, a, b])
+
+    @pl.loop(0, 2)
+    def _(half):
+        pl.loop(0, 2)(lambda n: dft(3, 2 * half + n))
+
+        @pl.when(half == 0)
         def _():
-            send(2, lambda other: outbox.at[2, other], inbox.at[2, a, b])
-
-        @pl.when(j == 3)
+            send(3, lambda other: outbox.at[3, other, low], early.at[a, b], 3)
+
+        @pl.when(half == 1)
         def _():
-            send(3, lambda other: outbox.at[3, other], last.at[a, b])
+            send(3, lambda other: outbox.at[3, other, high], last.at[a, b], 4)
 
     owns = [
-        pltpu.make_async_copy(
-            outbox.at[j, me], inbox.at[j, a, b] if j < 3 else last.at[a, b], own_sems.at[j]
-        )
-        for j in range(GROUPS)
+        pltpu.make_async_copy(outbox.at[j, me], inbox.at[j, a, b], own_sems.at[j])
+        for j in range(3)
+    ] + [
+        pltpu.make_async_copy(outbox.at[3, me, low], early.at[a, b], own_sems.at[3]),
+        pltpu.make_async_copy(outbox.at[3, me, high], last.at[a, b], own_sems.at[4]),
     ]
     for own in owns:
         own.start()
@@ -275,21 +300,22 @@
     def _():
         forward.wait_send()
 
-    def arrived(j):
-        some = outbox.at[j, pl.ds(0, DEVICES - 1)]
+    def arrived(j, some):
         pltpu.make_async_copy(some, some, recv_sems.at[j]).wait()
 
-    for j in range(3):
-        owns[j].wait()
+    for own in owns:
+        own.wait()
 
     @pl.loop(0, 3)
     def _(j):
-        arrived(j)
-
-        correlate_channel(inbox.at[j], rows, swapped, scale_col, scale_row, done.at[j])
-
-    owns[3].wait()
-    arrived(3)
+        arrived(j, outbox.at[j, pl.ds(0, DEVICES - 1)])
+        box = inbox.at[j]
+        halves = [box.at[:, :, low], box.at[:, :, high]]
+        correlate_channel(halves, rows, swapped, scale_col, scale_row, done.at[j])
+
+    arrived(3, outbox.at[3, pl.ds(0, DEVICES - 1), low])
+    correlate_channel([early], rows, swapped, scale_col, scale_row, None, held)
+    arrived(4, outbox.at[3, pl.ds(0, DEVICES - 1), high])
 
     @pl.loop(0, GROUPS)
     def _(j):
@@ -299,18 +325,20 @@
 
 def channelize(voltages, prototype, table):
     piece = (INP, TM, QUARTERS, 2 * PAIRS, 128)
+    half = (INP, TM, 2, 2 * PAIRS, 128)
     return pl.pallas_call(
         channelize_kernel,
         out_shape=(
             pltpu.VMEM((3, 2, INPUTS, INPUTS), jnp.bfloat16),
-            pltpu.VMEM(piece, jnp.bfloat16),
+            pltpu.VMEM((len(TILES), 2, TILE, TILE), jnp.float32),
+            pltpu.VMEM(half, jnp.bfloat16),
         ),
         in_specs=[
             pl.BlockSpec(memory_space=pl.ANY),
             pl.BlockSpec(memory_space=pltpu.VMEM),
             pl.BlockSpec(memory_space=pl.ANY),
         ],
-        out_specs=(pl.BlockSpec(memory_space=pltpu.VMEM), pl.BlockSpec(memory_space=pltpu.VMEM)),
+        out_specs=(pl.BlockSpec(memory_space=pltpu.VMEM),) * 3,
         scratch_shapes=[
             pltpu.VMEM((INPUTS_DEV, (SPEC_DEV + HALO) * FRAME), jnp.bfloat16),
             pltpu.VMEM((GROUPS, 2 * DEVICES, FRAME), jnp.bfloat16),
@@ -318,26 +346,27 @@
             pltpu.VMEM((2 * DEVICES * STRIDE, 128), jnp.float32),
             pltpu.VMEM((GROUPS, DEVICES, QUARTERS, 2 * PAIRS, 128), jnp.bfloat16),
             pltpu.VMEM((3, *piece), jnp.bfloat16),
+            pltpu.VMEM(half, jnp.bfloat16),
             pltpu.VMEM((INPUTS, INPUTS), jnp.bfloat16),
             pltpu.VMEM((INPUTS, INPUTS), jnp.bfloat16),
             pltpu.VMEM((INPUTS, 128), jnp.float32),
             pltpu.VMEM((1, INPUTS), jnp.float32),
             pltpu.SemaphoreType.DMA((3,)),
             pltpu.SemaphoreType.DMA,
-            pltpu.SemaphoreType.DMA((GROUPS,)),
+            pltpu.SemaphoreType.DMA((GROUPS + 1,)),
             pltpu.SemaphoreType.DMA((4,)),
             pltpu.SemaphoreType.DMA((GROUPS,)),
-            pltpu.SemaphoreType.DMA((GROUPS,)),
+            pltpu.SemaphoreType.DMA((GROUPS + 1,)),
             pltpu.SemaphoreType.REGULAR,
         ],
         compiler_params=pltpu.CompilerParams(
-            collective_id=0, has_side_effects=True, vmem_limit_bytes=43 * 1024 * 1024
+            collective_id=0, has_side_effects=True, vmem_limit_bytes=44 * 1024 * 1024
         ),
         name="channelize",
     )(voltages, prototype, table)
 
 
-def finish_kernel(done, last, o_hbm, rows, swapped, scale_col, scale_row, staged, sems):
+def finish_kernel(done, held, last, o_hbm, rows, swapped, scale_col, scale_row, staged, sems):
     copies = [pltpu.make_async_copy(done.at[c], o_hbm.at[c], sems.at[c]) for c in range(3)]
     for copy in copies:
         copy.start()
@@ -349,20 +378,20 @@
         )
         copies[-1].start()
 
-    correlate_channel(last, rows, swapped, scale_col, scale_row, staged, finished)
+    correlate_channel([last], rows, swapped, scale_col, scale_row, staged, held, finished)
     for copy in copies:
         copy.wait()
 
 
-def finish(done, last):
+def finish(done, held, last):
     return pl.pallas_call(
         finish_kernel,
         out_shape=jax.ShapeDtypeStruct((GROUPS, 2, INPUTS, INPUTS), jnp.bfloat16),
-        in_specs=[pl.BlockSpec(memory_space=pltpu.VMEM)] * 2,
+        in_specs=[pl.BlockSpec(memory_space=pltpu.VMEM)] * 3,
         out_specs=pl.BlockSpec(memory_space=pl.ANY),
         scratch_shapes=[
-            pltpu.VMEM((INPUTS, INPUTS), jnp.bfloat16),
-            pltpu.VMEM((INPUTS, INPUTS), jnp.bfloat16),
+            pltpu.VMEM((INPUTS, INPUTS // 2), jnp.bfloat16),
+            pltpu.VMEM((INPUTS, INPUTS // 2), jnp.bfloat16),
             pltpu.VMEM((INPUTS, 128), jnp.float32),
             pltpu.VMEM((1, INPUTS), jnp.float32),
             pltpu.VMEM((2, INPUTS, INPUTS), jnp.bfloat16),
@@ -370,7 +399,7 @@
         ],
         compiler_params=pltpu.CompilerParams(vmem_limit_bytes=20 * 1024 * 1024),
         name="finish",
-    )(done, last)
+    )(done, held, last)
 
 
 def shards(voltages, prototype):

time: 122 us -> 122 us (level)
  no operation moved by 1% of the time
where the time goes in v7:
time: 122 us
  Pallas kernels  122 us (100%)
    pallas_call x1, Pallas kernels, channelize(): pl.pallas_call(channelize_kernel, out_shape=(pltpu.VMEM((3, 2, INPUTS, IN...  116 us
    pallas_call x1, Pallas kernels, finish(): pl.pallas_call(finish_kernel, out_shape=jax.ShapeDtypeStruct((GROUPS, 2,...  5.91 us

profile of v7, /device:TPU:1, one launch (start us, length us, event | category | flops | bytes accessed | tf_op | source)
XLA Modules:
  0.0 121.5 jit_solution(14717972417604385073)
XLA Ops:
  0.0 115.6 %channelize.1 = (bf16[3,2,1024,1024]{3,2,1,0:T(8,128)(2,1)S(1)}, f32[10,2,256,256]{3,2,1,0:T(8,128)S(1)}, bf16[16,8,2,16,128]{4,3,2,1,0:T(8,128)(2,1)S(1)}) custom-call(bf16[64,65536]{1,0:T(8,128)(2,1)} %v_hbm.1, f32[8,1024]{1,0:T(8,128)} %proto_ref.1, bf16[4,256,1024]{2,1,0:T(8,128)(2,1)} %constant.2.clone.table_hbm), custom_call_target="tpu_custom_call" | custom-call | tf_op jit(solution)/shard_map/channelize/pallas_call | solution.py:329
  115.6 5.9 %finish.1 = bf16[4,2,1024,1024]{3,2,1,0:T(8,128)(2,1)} custom-call(bf16[3,2,1024,1024]{3,2,1,0:T(8,128)(2,1)S(1)} %get-tuple-element.8.done, f32[10,2,256,256]{3,2,1,0:T(8,128)S(1)} %get-tuple-element.9.held, bf16[16,8,2,16,128]{4,3,2,1,0:T(8,128)(2,1)S(1)} %get-tuple-element.10.last), custom_call_target="tpu_custom_call" | custom-call | tf_op jit(solution)/shard_map/finish/pallas_call | solution.py:387

commit v8 on v7

--- a/solution.py
+++ b/solution.py
@@ -132,12 +132,12 @@
         pltpu.make_async_copy(
             v_hbm.at[:, frames(first, count)], v.at[:, frames(BEFORE + first, count)], v_sems.at[n]
         )
-        for n, (first, count) in enumerate(((12, 24), (36, 28), (0, 12)))
+        for n, (first, count) in enumerate(
+            ((SPEC_DEV - BEFORE, BEFORE), (0, AFTER), (12, 24), (36, 24), (AFTER, 9))
+        )
     ]
-    for load in loads:
+    for load in loads[:2]:
         load.start()
-    table_load = pltpu.make_async_copy(table_hbm, table, table_sem)
-    table_load.start()
 
     def place(k):
         other = lax.rem(me + k * 37, DEVICES)
@@ -157,6 +157,10 @@
             )
 
     signal_row(barrier)
+    for load in loads[2:]:
+        load.start()
+    table_load = pltpu.make_async_copy(table_hbm, table, table_sem)
+    table_load.start()
 
     def fir(chunk, q, last=False):
         at = pl.ds(pl.multiple_of(q * 16, 16), 16)
@@ -215,10 +219,8 @@
 
     forward = halo(SPEC_DEV, BEFORE, 0, 1, 0)
     back = halo(BEFORE, AFTER, BEFORE + SPEC_DEV, TM - 1, 1)
-    loads[0].wait()
-    pl.loop(0, 4)(lambda q: fir(2, q))
-    loads[1].wait()
-    loads[2].wait()
+    for load in loads[:2]:
+        load.wait()
     pl.semaphore_wait(barrier, INP + TM - 2)
     back.start()
 
@@ -227,8 +229,10 @@
         forward.start()
 
     signal_row(row_sem)
-
-    pl.loop(0, 4)(lambda q: fir(3, q))
+    loads[2].wait()
+    pl.loop(0, 8)(lambda t: fir(2 + lax.div(t, 4), lax.rem(t, 4)))
+    for load in loads[3:]:
+        load.wait()
     table_load.wait()
     pl.semaphore_wait(row_sem, TM - 1)
 
@@ -351,7 +355,7 @@
             pltpu.VMEM((INPUTS, INPUTS), jnp.bfloat16),
             pltpu.VMEM((INPUTS, 128), jnp.float32),
             pltpu.VMEM((1, INPUTS), jnp.float32),
-            pltpu.SemaphoreType.DMA((3,)),
+            pltpu.SemaphoreType.DMA((5,)),
             pltpu.SemaphoreType.DMA,
             pltpu.SemaphoreType.DMA((GROUPS + 1,)),
             pltpu.SemaphoreType.DMA((4,)),

time: 122 us -> 121 us (level)
  no operation moved by 1% of the time
where the time goes in v8:
time: 121 us
  Pallas kernels  121 us (100%)
    pallas_call x1, Pallas kernels, channelize(): pl.pallas_call(channelize_kernel, out_shape=(pltpu.VMEM((3, 2, INPUTS, IN...  115 us
    pallas_call x1, Pallas kernels, finish(): pl.pallas_call(finish_kernel, out_shape=jax.ShapeDtypeStruct((GROUPS, 2,...  5.91 us

profile of v8, /device:TPU:1, one launch (start us, length us, event | category | flops | bytes accessed | tf_op | source)
XLA Modules:
  0.0 120.8 jit_solution(5486294860268046314)
XLA Ops:
  0.0 114.8 %channelize.1 = (bf16[3,2,1024,1024]{3,2,1,0:T(8,128)(2,1)S(1)}, f32[10,2,256,256]{3,2,1,0:T(8,128)S(1)}, bf16[16,8,2,16,128]{4,3,2,1,0:T(8,128)(2,1)S(1)}) custom-call(bf16[64,65536]{1,0:T(8,128)(2,1)} %v_hbm.1, f32[8,1024]{1,0:T(8,128)} %proto_ref.1, bf16[4,256,1024]{2,1,0:T(8,128)(2,1)} %constant.2.clone.table_hbm), custom_call_target="tpu_custom_call" | custom-call | tf_op jit(solution)/shard_map/channelize/pallas_call | solution.py:333
  114.8 5.9 %finish.1 = bf16[4,2,1024,1024]{3,2,1,0:T(8,128)(2,1)} custom-call(bf16[3,2,1024,1024]{3,2,1,0:T(8,128)(2,1)S(1)} %get-tuple-element.8.done, f32[10,2,256,256]{3,2,1,0:T(8,128)S(1)} %get-tuple-element.9.held, bf16[16,8,2,16,128]{4,3,2,1,0:T(8,128)(2,1)S(1)} %get-tuple-element.10.last), custom_call_target="tpu_custom_call" | custom-call | tf_op jit(solution)/shard_map/finish/pallas_call | solution.py:391

commit v9 on v8

--- a/solution.py
+++ b/solution.py
@@ -347,7 +347,7 @@
             pltpu.VMEM((INPUTS_DEV, (SPEC_DEV + HALO) * FRAME), jnp.bfloat16),
             pltpu.VMEM((GROUPS, 2 * DEVICES, FRAME), jnp.bfloat16),
             pltpu.VMEM((SPEC_DEV, INPUTS_DEV, FRAME), jnp.bfloat16),
-            pltpu.VMEM((2 * DEVICES * STRIDE, 128), jnp.float32),
+            pltpu.VMEM((2 * DEVICES * STRIDE + 16, 128), jnp.float32),
             pltpu.VMEM((GROUPS, DEVICES, QUARTERS, 2 * PAIRS, 128), jnp.bfloat16),
             pltpu.VMEM((3, *piece), jnp.bfloat16),
             pltpu.VMEM(half, jnp.bfloat16),

time: 121 us -> 121 us (level)
  no operation moved by 1% of the time
where the time goes in v9:
time: 121 us
  Pallas kernels  121 us (100%)
    pallas_call x1, Pallas kernels, channelize(): pl.pallas_call(channelize_kernel, out_shape=(pltpu.VMEM((3, 2, INPUTS, IN...  115 us
    pallas_call x1, Pallas kernels, finish(): pl.pallas_call(finish_kernel, out_shape=jax.ShapeDtypeStruct((GROUPS, 2,...  5.91 us

profile of v9, /device:TPU:1, one launch (start us, length us, event | category | flops | bytes accessed | tf_op | source)
XLA Modules:
  0.0 120.8 jit_solution(12190787022266465006)
XLA Ops:
  0.0 114.8 %channelize.1 = (bf16[3,2,1024,1024]{3,2,1,0:T(8,128)(2,1)S(1)}, f32[10,2,256,256]{3,2,1,0:T(8,128)S(1)}, bf16[16,8,2,16,128]{4,3,2,1,0:T(8,128)(2,1)S(1)}) custom-call(bf16[64,65536]{1,0:T(8,128)(2,1)} %v_hbm.1, f32[8,1024]{1,0:T(8,128)} %proto_ref.1, bf16[4,256,1024]{2,1,0:T(8,128)(2,1)} %constant.2.clone.table_hbm), custom_call_target="tpu_custom_call" | custom-call | tf_op jit(solution)/shard_map/channelize/pallas_call | solution.py:333
  114.8 5.9 %finish.1 = bf16[4,2,1024,1024]{3,2,1,0:T(8,128)(2,1)} custom-call(bf16[3,2,1024,1024]{3,2,1,0:T(8,128)(2,1)S(1)} %get-tuple-element.8.done, f32[10,2,256,256]{3,2,1,0:T(8,128)S(1)} %get-tuple-element.9.held, bf16[16,8,2,16,128]{4,3,2,1,0:T(8,128)(2,1)S(1)} %get-tuple-element.10.last), custom_call_target="tpu_custom_call" | custom-call | tf_op jit(solution)/shard_map/finish/pallas_call | solution.py:391
